TPU v7x, 32 devices: a whole 2x2x4 slice. The times are simulated.
32 devices in a mesh: dp: 8 (over z, y), mp: 4 (over x, core).
Axes of the slice: x: 2, y: 2, z: 4, core: 2. Of those that a mesh axis runs over, the one named last changes fastest.
Arguments:
- tokens: bfloat16 [8192, 768], P('dp'), may hold values from -6 to 6
- noise_field: bfloat16 [8192, 768], P('dp'), may hold values from -6 to 6
- codec_tokens: bfloat16 [16, 256, 768], P('dp'), may hold values from -6 to 6
- timesteps: int32 [16], P('dp'), may hold values from 0 to 999
- segments: int32 [16, 512], P('dp'), may hold values from 0 to 3, never falling along the last dimension, each value on 1 to 256 neighbouring positions
- cotangent: bfloat16 [8192, 768], P('dp'), may hold values from -6 to 6
- w_in: float32 [16, 768, 768], P(None, 'dp', 'mp'), may hold values from -0.14433757 to 0.14433757
- w_back: float32 [11, 768, 768], P(None, 'mp', 'dp'), may hold values from -0.4082483 to 0.4082483
- w_up: float32 [768, 3072], P('dp', 'mp'), may hold values from -0.21875 to 0.21875
- w_down: float32 [3072, 768], P('mp', 'dp'), may hold values from -0.109375 to 0.109375
- m_in: float32 [16, 768, 768], P(None, 'dp', 'mp'), may hold values from -256 to 256
- m_back: float32 [11, 768, 768], P(None, 'mp', 'dp'), may hold values from -256 to 256
- m_up: float32 [768, 3072], P('dp', 'mp'), may hold values from -256 to 256
- m_down: float32 [3072, 768], P('mp', 'dp'), may hold values from -256 to 256
- v_in: float32 [16, 768, 768], P(None, 'dp', 'mp'), may hold values from 2048 to 8192
- v_back: float32 [11, 768, 768], P(None, 'mp', 'dp'), may hold values from 2048 to 8192
- v_up: float32 [768, 3072], P('dp', 'mp'), may hold values from 2048 to 8192
- v_down: float32 [3072, 768], P('mp', 'dp'), may hold values from 2048 to 8192
- norm_params: float32 [10, 768], replicated, may hold values from -1.2 to 1.4
- norm_m: float32 [10, 768], replicated, may hold values from -256 to 256
- norm_v: float32 [10, 768], replicated, may hold values from 2048 to 8192
Outputs:
- out: bfloat16 [8192, 768], P('dp')
- grad_x: float32 [8192, 768], P('dp')
- new_w_in: float32 [16, 768, 768], P(None, 'dp', 'mp')
- new_w_back: float32 [11, 768, 768], P(None, 'mp', 'dp')
- new_w_up: float32 [768, 3072], P('dp', 'mp')
- new_w_down: float32 [3072, 768], P('mp', 'dp')
- new_m_in: float32 [16, 768, 768], P(None, 'dp', 'mp')
- new_m_back: float32 [11, 768, 768], P(None, 'mp', 'dp')
- new_m_up: float32 [768, 3072], P('dp', 'mp')
- new_m_down: float32 [3072, 768], P('mp', 'dp')
- new_v_in: float32 [16, 768, 768], P(None, 'dp', 'mp')
- new_v_back: float32 [11, 768, 768], P(None, 'mp', 'dp')
- new_v_up: float32 [768, 3072], P('dp', 'mp')
- new_v_down: float32 [3072, 768], P('mp', 'dp')
- new_norm_params: float32 [10, 768], replicated
- new_norm_m: float32 [10, 768], replicated
- new_norm_v: float32 [10, 768], replicated
- matrix_norms: float32 [2, 29], replicated
Inputs may be any that keep to these rules, and one draw needn't show every extreme that they name: `segments`: along a sequence segment ids never fall; patches attend only within their segment; a segment holds at most 256 patches.
All inputs are finite; a program needn't handle non-finite values.
Results may differ from a plain program's by a relative error of at most 0.015.
Values may be sent and summed in bfloat16 or wider, within the bound.
A program may use at most 256 MiB of HBM per device.

v0:
```python
from functools import partial
import math

import jax
import jax.numpy as jnp
from jax import lax
from jax.experimental import pallas as pl
from jax.experimental.pallas import tpu as pltpu
from jax.sharding import PartitionSpec as P

HD = 64
GROUPS = 32
FREQ = 8
TIME = 64
TSTEPS = 1000
STEP = 5


NORM_EPS = 1e-05
MOMENT_DECAY = 0.5
LEARN_RATE = 0.5
WEIGHT_DECAY = 0.01
ADAM_EPS = 1e-06
MASK_VALUE = -1e30
HIGHEST_PRECISION = lax.Precision.HIGHEST


def layer_norm(value_tensor, gain_row, shift_row):
    centre = value_tensor - jnp.mean(value_tensor, axis=-1, keepdims=True)
    spread = jnp.mean(centre * centre, axis=-1, keepdims=True)
    return centre * lax.rsqrt(spread + NORM_EPS) * gain_row + shift_row


def group_norm(value_tensor, gain_row, shift_row, group_width):
    seqs_here, length, channels = value_tensor.shape
    grouped = value_tensor.reshape(seqs_here, length, channels // group_width, group_width)
    centre = grouped - jnp.mean(grouped, axis=(1, 3), keepdims=True)
    spread = jnp.mean(centre * centre, axis=(1, 3), keepdims=True)
    normed = (centre * lax.rsqrt(spread + NORM_EPS)).reshape(seqs_here, length, channels)
    return normed * gain_row + shift_row


def norm_silu(value_tensor, gain_row, shift_row, group_width):
    return jax.nn.silu(group_norm(value_tensor, gain_row, shift_row, group_width))


def time_embedding(timesteps, features):
    half_width = features // 2
    freq_rates = jnp.exp(
        -math.log(10000.0) * jnp.arange(half_width, dtype=jnp.float32) / half_width
    )
    angles = timesteps.astype(jnp.float32)[:, None] * freq_rates[None, :]
    return jnp.concatenate([jnp.sin(angles), jnp.cos(angles)], axis=1)


def flatten_rows(value_tensor):
    return value_tensor.reshape(-1, value_tensor.shape[-1])


def project(values_low, weight_matrix):
    summed = jnp.dot(flatten_rows(values_low), weight_matrix, preferred_element_type=jnp.float32)
    return summed.reshape(values_low.shape[0], values_low.shape[1], weight_matrix.shape[1])


def back_project(grad_low, weight_matrix):
    summed = jnp.einsum(
        "ne,ce->nc", flatten_rows(grad_low), weight_matrix, preferred_element_type=jnp.float32
    )
    return summed.reshape(grad_low.shape[0], grad_low.shape[1], weight_matrix.shape[0])


def weight_grad(left_low, right_low):
    return jnp.einsum(
        "nc,ne->ce",
        flatten_rows(left_low),
        flatten_rows(right_low),
        preferred_element_type=jnp.float32,
    )


def padded_grid(grid_rows):
    seqs_here = grid_rows.shape[0]
    return jnp.pad(grid_rows.reshape(seqs_here, FREQ, TIME, -1), ((0, 0), (1, 1), (1, 1), (0, 0)))


def grid_window(padded, tap_index):
    row_off = tap_index // 3
    col_off = tap_index % 3
    return padded[:, row_off : row_off + FREQ, col_off : col_off + TIME, :].reshape(
        -1, padded.shape[3]
    )


def conv_grid(grid_rows, tap_weights, backward):
    seqs_here = grid_rows.shape[0]
    padded = padded_grid(grid_rows)
    out_width = tap_weights.shape[1] if backward else tap_weights.shape[2]
    summed = jnp.zeros((seqs_here * FREQ * TIME, out_width), jnp.float32)
    for tap_index in range(9):
        window = grid_window(padded, tap_index)
        if backward:
            summed = summed + jnp.einsum(
                "nc,dc->nd", window, tap_weights[8 - tap_index], preferred_element_type=jnp.float32
            )
        else:
            summed = summed + jnp.dot(
                window, tap_weights[tap_index], preferred_element_type=jnp.float32
            )
    return summed.reshape(seqs_here, FREQ * TIME, out_width)


def conv_weight_grad(grid_low, grad_low):
    padded = padded_grid(grid_low)
    grad_flat = flatten_rows(grad_low)
    tap_grads = []
    for tap_index in range(9):
        window = grid_window(padded, tap_index)
        tap_grads.append(
            jnp.einsum("nc,ne->ce", window, grad_flat, preferred_element_type=jnp.float32)
        )
    return jnp.stack(tap_grads)


def split_heads(rows_low):
    return rows_low.reshape(rows_low.shape[0], rows_low.shape[1], rows_low.shape[2] // HD, HD)


def head_scores(queries, key_rows, allowed, score_scale):
    scores = (
        jnp.einsum(
            "sqhd,skhd->shqk",
            split_heads(queries),
            split_heads(key_rows),
            preferred_element_type=jnp.float32,
        )
        * score_scale
    )
    if allowed is not None:
        scores = jnp.where(allowed[:, None], scores, MASK_VALUE)
    return scores


def attend(queries, key_rows, value_rows, allowed, score_scale):
    scores = head_scores(queries, key_rows, allowed, score_scale)
    highest = jnp.max(scores, axis=-1, keepdims=True)
    raised = jnp.exp(scores - highest)
    totals = jnp.sum(raised, axis=-1, keepdims=True)
    soft_low = (raised / totals).astype(jnp.bfloat16)
    mixed_rows = jnp.einsum(
        "shqk,skhd->sqhd", soft_low, split_heads(value_rows), preferred_element_type=jnp.float32
    )
    return (mixed_rows.reshape(queries.shape), highest + jnp.log(totals))


def attend_back(queries, key_rows, value_rows, allowed, score_scale, log_total, grad_mixed):
    scores = head_scores(queries, key_rows, allowed, score_scale)
    soft = jnp.exp(scores - log_total)
    grad_heads = split_heads(grad_mixed)
    grad_soft = jnp.einsum(
        "sqhd,skhd->shqk", grad_heads, split_heads(value_rows), preferred_element_type=jnp.float32
    )
    grad_values = jnp.einsum(
        "shqk,sqhd->skhd", soft.astype(jnp.bfloat16), grad_heads, preferred_element_type=jnp.float32
    )
    row_dot = jnp.sum(soft * grad_soft, axis=-1, keepdims=True)
    grad_scores = (soft * (grad_soft - row_dot)).astype(jnp.bfloat16)
    grad_queries = (
        jnp.einsum(
            "shqk,skhd->sqhd",
            grad_scores,
            split_heads(key_rows),
            preferred_element_type=jnp.float32,
        )
        * score_scale
    )
    grad_keys = (
        jnp.einsum(
            "shqk,sqhd->skhd", grad_scores, split_heads(queries), preferred_element_type=jnp.float32
        )
        * score_scale
    )
    return (
        grad_queries.reshape(queries.shape).astype(jnp.bfloat16),
        grad_keys.reshape(key_rows.shape).astype(jnp.bfloat16),
        grad_values.reshape(value_rows.shape).astype(jnp.bfloat16),
    )


def tensor_parallel_sum(term_rows):
    return lax.psum(term_rows, "mp")


def matrix_squares(first_stack, second_stack, up_rows, down_rows):
    return jnp.concatenate(
        [
            jnp.sum(first_stack * first_stack, axis=(1, 2)),
            jnp.sum(second_stack * second_stack, axis=(1, 2)),
            jnp.sum(up_rows * up_rows)[None],
            jnp.sum(down_rows * down_rows)[None],
        ]
    )


def adam_update(master, grad_rows, first_moment, second_moment, decay_rate):
    first_new = MOMENT_DECAY * first_moment + (1.0 - MOMENT_DECAY) * grad_rows
    second_new = MOMENT_DECAY * second_moment + (1.0 - MOMENT_DECAY) * grad_rows * grad_rows
    correct = 1.0 - MOMENT_DECAY**STEP
    update = first_new / correct / (jnp.sqrt(second_new / correct) + ADAM_EPS) + decay_rate * master
    return (first_new, second_new, update)


def generic_device(
    tokens,
    noise_field,
    codec_tokens,
    timesteps,
    segments,
    cotangent,
    w_in,
    w_back,
    w_up,
    w_down,
    m_in,
    m_back,
    m_up,
    m_down,
    v_in,
    v_back,
    v_up,
    v_down,
    norm_params,
    norm_m,
    norm_v,
):
    seqs_here, length = segments.shape
    features = tokens.shape[1]
    chans_here = w_in.shape[2]
    group_width = features // GROUPS
    score_scale = HD ** (-0.5)
    channel_start = lax.axis_index("mp") * chans_here
    lead_device = (lax.axis_index("mp") == 0).astype(jnp.float32)
    weight_sq = matrix_squares(w_in, w_back, w_up, w_down)
    full_in, full_back, complete_up_weight, full_down = (
        lax.all_gather(w_in.astype(jnp.bfloat16), "dp", axis=1, tiled=True),
        lax.all_gather(w_back.astype(jnp.bfloat16), "dp", axis=2, tiled=True),
        lax.all_gather(w_up.astype(jnp.bfloat16), "dp", axis=0, tiled=True),
        lax.all_gather(w_down.astype(jnp.bfloat16), "dp", axis=1, tiled=True),
    )
    resid_in = tokens.astype(jnp.float32).reshape(seqs_here, length, features)
    allowed = segments[:, :, None] == segments[:, None, :]
    normed_one_low = layer_norm(resid_in, norm_params[0], norm_params[1]).astype(jnp.bfloat16)
    queries = project(normed_one_low, full_in[0]).astype(jnp.bfloat16)
    key_rows = project(normed_one_low, full_in[1]).astype(jnp.bfloat16)
    value_rows = project(normed_one_low, full_in[2]).astype(jnp.bfloat16)
    mixed_rows, log_self = attend(queries, key_rows, value_rows, allowed, score_scale)
    mixed_low = mixed_rows.astype(jnp.bfloat16)
    resid_one = resid_in + tensor_parallel_sum(project(mixed_low, full_back[0]))
    normed_two_low = layer_norm(resid_one, norm_params[2], norm_params[3]).astype(jnp.bfloat16)
    hidden_pre = project(normed_two_low, complete_up_weight)
    hidden_low = jax.nn.gelu(hidden_pre).astype(jnp.bfloat16)
    resid_two = resid_one + tensor_parallel_sum(project(hidden_low, full_down))
    noise_level = jnp.sqrt((timesteps.astype(jnp.float32) + 1.0) / TSTEPS)
    noisy = resid_two + noise_level[:, None, None] * noise_field.astype(jnp.float32).reshape(
        seqs_here, length, features
    )
    first_low = norm_silu(noisy, norm_params[4], norm_params[5], group_width).astype(jnp.bfloat16)
    embed_low = jax.nn.silu(time_embedding(timesteps, features)).astype(jnp.bfloat16)
    time_shift = jnp.dot(embed_low, full_in[3], preferred_element_type=jnp.float32)
    conv_one = conv_grid(first_low, full_in[7:16], False) + time_shift[:, None, :]
    gain_six = lax.dynamic_slice_in_dim(norm_params[6], channel_start, chans_here)
    shift_six = lax.dynamic_slice_in_dim(norm_params[7], channel_start, chans_here)
    second_low = norm_silu(conv_one, gain_six, shift_six, group_width).astype(jnp.bfloat16)
    resid_three = noisy + tensor_parallel_sum(conv_grid(second_low, full_back[2:11], False))
    normed_three_low = layer_norm(resid_three, norm_params[8], norm_params[9]).astype(jnp.bfloat16)
    cross_queries = project(normed_three_low, full_in[4]).astype(jnp.bfloat16)
    cross_keys = project(codec_tokens, full_in[5]).astype(jnp.bfloat16)
    cross_values = project(codec_tokens, full_in[6]).astype(jnp.bfloat16)
    cross_mixed, log_cross = attend(cross_queries, cross_keys, cross_values, None, score_scale)
    cross_low = cross_mixed.astype(jnp.bfloat16)
    result = resid_three + tensor_parallel_sum(project(cross_low, full_back[1]))
    out_low = result.astype(jnp.bfloat16)
    grad_out = cotangent.astype(jnp.float32).reshape(seqs_here, length, features)
    grad_cross_low = grad_out.astype(jnp.bfloat16)
    grad_w_co = weight_grad(cross_low, grad_cross_low)
    grad_cross_mixed = back_project(grad_cross_low, full_back[1]).astype(jnp.bfloat16)
    grad_cq, grad_ck, grad_cv = attend_back(
        cross_queries, cross_keys, cross_values, None, score_scale, log_cross, grad_cross_mixed
    )
    grad_w_cq = weight_grad(normed_three_low, grad_cq)
    grad_w_ck = weight_grad(codec_tokens, grad_ck)
    grad_w_cv = weight_grad(codec_tokens, grad_cv)
    grad_normed_three = tensor_parallel_sum(back_project(grad_cq, full_in[4]))
    pull_three = jax.vjp(layer_norm, resid_three, norm_params[8], norm_params[9])[1]
    grad_part, grad_gain_eight, grad_shift_eight = pull_three(grad_normed_three)
    grad_three = grad_out + grad_part
    grad_conv_low = grad_three.astype(jnp.bfloat16)
    grad_w_conv_two = conv_weight_grad(second_low, grad_conv_low)
    grad_second = conv_grid(grad_conv_low, full_back[2:11], True)
    gather_second_moment = jax.vjp(
        partial(norm_silu, group_width=group_width), conv_one, gain_six, shift_six
    )[1]
    grad_conv_one, grad_gain_six, grad_shift_six = gather_second_moment(grad_second)
    grad_conv_one_low = grad_conv_one.astype(jnp.bfloat16)
    grad_w_time = jnp.einsum(
        "sd,sc->dc",
        embed_low.astype(jnp.float32),
        jnp.sum(grad_conv_one_low.astype(jnp.float32), axis=1),
        precision=HIGHEST_PRECISION,
    )
    grad_w_conv_one = conv_weight_grad(first_low, grad_conv_one_low)
    grad_first = tensor_parallel_sum(conv_grid(grad_conv_one_low, full_in[7:16], True))
    gather_first_moment = jax.vjp(
        partial(norm_silu, group_width=group_width), noisy, norm_params[4], norm_params[5]
    )[1]
    grad_part, grad_gain_four, grad_shift_four = gather_first_moment(grad_first)
    grad_two = grad_three + grad_part
    grad_mlp_low = grad_two.astype(jnp.bfloat16)
    grad_w_down = weight_grad(hidden_low, grad_mlp_low)
    grad_hidden = back_project(grad_mlp_low, full_down)
    grad_pre_low = jax.vjp(jax.nn.gelu, hidden_pre)[1](grad_hidden)[0].astype(jnp.bfloat16)
    up_weight_gradient = weight_grad(normed_two_low, grad_pre_low)
    grad_normed_two = tensor_parallel_sum(back_project(grad_pre_low, complete_up_weight))
    pull_two = jax.vjp(layer_norm, resid_one, norm_params[2], norm_params[3])[1]
    grad_part, grad_gain_two, grad_shift_two = pull_two(grad_normed_two)
    grad_one = grad_two + grad_part
    grad_attn_low = grad_one.astype(jnp.bfloat16)
    grad_w_out = weight_grad(mixed_low, grad_attn_low)
    grad_mixed = back_project(grad_attn_low, full_back[0]).astype(jnp.bfloat16)
    grad_q, grad_k, grad_v = attend_back(
        queries, key_rows, value_rows, allowed, score_scale, log_self, grad_mixed
    )
    grad_w_q = weight_grad(normed_one_low, grad_q)
    grad_w_k = weight_grad(normed_one_low, grad_k)
    grad_w_v = weight_grad(normed_one_low, grad_v)
    grad_normed_one = tensor_parallel_sum(
        back_project(grad_q, full_in[0])
        + back_project(grad_k, full_in[1])
        + back_project(grad_v, full_in[2])
    )
    pull_one = jax.vjp(layer_norm, resid_in, norm_params[0], norm_params[1])[1]
    grad_part, grad_gain_zero, grad_shift_zero = pull_one(grad_normed_one)
    grad_input = grad_one + grad_part
    grad_in_stack = jnp.concatenate(
        [
            jnp.stack([grad_w_q, grad_w_k, grad_w_v, grad_w_time, grad_w_cq, grad_w_ck, grad_w_cv]),
            grad_w_conv_one,
        ]
    )
    grad_back_stack = jnp.concatenate([jnp.stack([grad_w_out, grad_w_co]), grad_w_conv_two])
    summed_in, summed_back, summed_up, summed_down = (
        lax.psum_scatter(grad_in_stack, "dp", scatter_dimension=1, tiled=True),
        lax.psum_scatter(grad_back_stack, "dp", scatter_dimension=2, tiled=True),
        lax.psum_scatter(up_weight_gradient, "dp", scatter_dimension=0, tiled=True),
        lax.psum_scatter(grad_w_down, "dp", scatter_dimension=1, tiled=True),
    )
    shared_rows = (
        jnp.stack(
            [
                grad_gain_zero,
                grad_shift_zero,
                grad_gain_two,
                grad_shift_two,
                grad_gain_four,
                grad_shift_four,
            ]
        )
        * lead_device
    )
    group_rows = lax.dynamic_update_slice(
        jnp.zeros((2, features), jnp.float32),
        jnp.stack([grad_gain_six, grad_shift_six]),
        (0, channel_start),
    )
    last_rows = jnp.stack([grad_gain_eight, grad_shift_eight]) * lead_device
    norm_grad = lax.psum(jnp.concatenate([shared_rows, group_rows, last_rows]), ("dp", "mp"))
    m_in_new, v_in_new, upd_in = adam_update(w_in, summed_in, m_in, v_in, WEIGHT_DECAY)
    m_back_new, v_back_new, upd_back = adam_update(
        w_back, summed_back, m_back, v_back, WEIGHT_DECAY
    )
    m_up_new, v_up_new, upd_up = adam_update(w_up, summed_up, m_up, v_up, WEIGHT_DECAY)
    m_down_new, v_down_new, upd_down = adam_update(
        w_down, summed_down, m_down, v_down, WEIGHT_DECAY
    )
    update_sq = matrix_squares(upd_in, upd_back, upd_up, upd_down)
    weight_total, update_total = lax.psum((weight_sq, update_sq), ("dp", "mp"))
    weight_len = jnp.sqrt(weight_total)
    update_len = jnp.sqrt(update_total)
    trust = weight_len / update_len
    new_in = w_in - LEARN_RATE * trust[0:16, None, None] * upd_in
    new_back = w_back - LEARN_RATE * trust[16:27, None, None] * upd_back
    new_up = w_up - LEARN_RATE * trust[27] * upd_up
    new_down = w_down - LEARN_RATE * trust[28] * upd_down
    norm_m_new, norm_v_new, upd_norm = adam_update(norm_params, norm_grad, norm_m, norm_v, 0.0)
    row_trust = jnp.sqrt(jnp.sum(norm_params * norm_params, axis=1)) / jnp.sqrt(
        jnp.sum(upd_norm * upd_norm, axis=1)
    )
    new_norm = norm_params - LEARN_RATE * row_trust[:, None] * upd_norm
    matrix_norms = jnp.stack([weight_len, update_len])
    out_rows = out_low.reshape(seqs_here * length, features)
    grad_rows = grad_input.reshape(seqs_here * length, features)
    return (
        out_rows,
        grad_rows,
        new_in,
        new_back,
        new_up,
        new_down,
        m_in_new,
        m_back_new,
        m_up_new,
        m_down_new,
        v_in_new,
        v_back_new,
        v_up_new,
        v_down_new,
        new_norm,
        norm_m_new,
        norm_v_new,
        matrix_norms,
    )


CORE_SWAP = [(i, i ^ 1) for i in range(4)]
X_SWAP = [(i, i ^ 2) for i in range(4)]
LOW = jnp.bfloat16
F32 = jnp.float32


def swap_core(v):
    return lax.ppermute(v, "mp", CORE_SWAP)


def swap_x(v):
    return lax.ppermute(v, "mp", X_SWAP)


def by_parity(flag, own, other, axis):
    first = jnp.where(flag == 0, own, other)
    second = jnp.where(flag == 0, other, own)
    return jnp.stack([first, second], axis=axis)


def pick(v, index, axis):
    return lax.dynamic_index_in_dim(v, index, axis, keepdims=False)


def ln_stats(v):
    centre = v - jnp.mean(v, axis=-1, keepdims=True)
    scale = lax.rsqrt(jnp.mean(centre * centre, axis=-1, keepdims=True) + NORM_EPS)
    return centre * scale, scale


def ln_back(v, gain, grad):
    hat, scale = ln_stats(v)
    pulled = grad * gain
    back = scale * (
        pulled
        - jnp.mean(pulled, axis=-1, keepdims=True)
        - hat * jnp.mean(pulled * hat, axis=-1, keepdims=True)
    )
    return back, jnp.sum(grad * hat, axis=0, keepdims=True), jnp.sum(grad, axis=0, keepdims=True)


def mm(a, b):
    return lax.dot_general(a, b, (((1,), (0,)), ((), ())), preferred_element_type=F32)


def mm_nt(a, b):
    return lax.dot_general(a, b, (((1,), (1,)), ((), ())), preferred_element_type=F32)


def mm_tn(a, b):
    return lax.dot_general(a, b, (((0,), (0,)), ((), ())), preferred_element_type=F32)


ANY = pl.ANY
VM = pltpu.VMEM
ROWS = 512
STEP_ROWS = 128


def spec_any():
    return pl.BlockSpec(memory_space=pl.ANY)


def spec_vm():
    return pl.BlockSpec(memory_space=pltpu.VMEM)


def run_kernel(body, name, ins, outs, scratch, hbm=(), flops=0):
    in_specs = [spec_any() if k in hbm else spec_vm() for k in range(len(ins))]
    moved = sum(v.size * v.dtype.itemsize for v in ins) + sum(
        math.prod(s) * jnp.dtype(t).itemsize for s, t in outs
    )
    return pl.pallas_call(
        body,
        name=name,
        in_specs=in_specs,
        out_specs=[spec_vm() for _ in outs],
        out_shape=[jax.ShapeDtypeStruct(s, t) for s, t in outs],
        scratch_shapes=scratch,
        compiler_params=pltpu.CompilerParams(vmem_limit_bytes=56 << 20),
        cost_estimate=pl.CostEstimate(flops=flops, bytes_accessed=moved, transcendentals=0),
    )(*ins)


def each_rows(fn, total=ROWS, step=STEP_ROWS):
    def body(k, carry):
        fn(pl.ds(pl.multiple_of(k * step, step), step))
        return carry

    lax.fori_loop(0, total // step, body, 0)


def start_copies(pairs, sems):
    copies = [pltpu.make_async_copy(a, b, sems.at[k]) for k, (a, b) in enumerate(pairs)]
    for c in copies:
        c.start()
    return copies


def group_mats(channels, width):
    count = channels // width
    r = lax.broadcasted_iota(jnp.int32, (channels, count), 0)
    c = lax.broadcasted_iota(jnp.int32, (channels, count), 1) * width
    down = ((r >= c) & (r < c + width)).astype(F32)
    r = lax.broadcasted_iota(jnp.int32, (count, channels), 1)
    c = lax.broadcasted_iota(jnp.int32, (count, channels), 0) * width
    up = ((r >= c) & (r < c + width)).astype(F32)
    return down, up


def exact_dot(a, b):
    return jnp.dot(a, b, precision=HIGHEST_PRECISION, preferred_element_type=F32)


def group_average(row, mats, width):
    wide = jnp.broadcast_to(row, (8, row.shape[1]))
    return exact_dot(exact_dot(wide, mats[0]) * (1.0 / (width * ROWS)), mats[1])[0:1]


def gelu_parts(v):
    k = math.sqrt(2.0 / math.pi)
    t = jnp.tanh(k * (v + 0.044715 * (v * v * v)))
    return t, 0.5 * v * (1.0 + t)


def gelu_slope(v, t):
    k = math.sqrt(2.0 / math.pi)
    return 0.5 * (1.0 + t) + 0.5 * v * (1.0 - t * t) * (k * (1.0 + 3 * 0.044715 * (v * v)))


def column_of(shape):
    return lax.broadcasted_iota(jnp.int32, shape, 0) % TIME


def from_left(v):
    return jnp.where(column_of(v.shape) == 0, 0.0, pltpu.roll(v, 1, 0))


def from_right(v):
    return jnp.where(column_of(v.shape) == TIME - 1, 0.0, pltpu.roll(v, v.shape[0] - 1, 0))


def softmax_heads(q, k, v, heads, score_scale, mask):
    mixed, logs = [], []
    for h in range(heads):
        s = mm_nt(q[:, HD * h : HD * (h + 1)], k[:, HD * h : HD * (h + 1)]) * score_scale
        if mask is not None:
            s = jnp.where(mask, s, MASK_VALUE)
        top = jnp.max(s, axis=1, keepdims=True)
        e = jnp.exp(s - top)
        total = jnp.sum(e, axis=1, keepdims=True)
        soft = (e * (1.0 / total)).astype(LOW)
        mixed.append(mm(soft, v[:, HD * h : HD * (h + 1)]))
        logs.append(top + jnp.log(total))
    return jnp.concatenate(mixed, axis=1).astype(LOW), logs


def softmax_heads_back(q, k, v, g, logs, heads, score_scale, mask):
    dq, dk, dv = [], [], []
    for h in range(heads):
        cols = slice(HD * h, HD * (h + 1))
        s = mm_nt(q[:, cols], k[:, cols]) * score_scale
        if mask is not None:
            s = jnp.where(mask, s, MASK_VALUE)
        soft = jnp.exp(s - logs[h])
        gs = mm_nt(g[:, cols], v[:, cols])
        dv.append(mm_tn(soft.astype(LOW), g[:, cols]))
        dot = jnp.sum(soft * gs, axis=1, keepdims=True)
        ds = (soft * (gs - dot)).astype(LOW)
        dq.append(mm(ds, k[:, cols]) * score_scale)
        dk.append(mm_tn(ds, q[:, cols]))
    return [jnp.concatenate(d, axis=1) for d in (dq, dk, dv)]


MESH_IDS = pl.DeviceIdType.MESH


def place():
    mp = lax.axis_index("mp")
    dp = lax.axis_index("dp")
    return mp // 2, mp % 2, dp // 2, dp % 2


def device(x, core, z, y):
    return (2 * z + y, 2 * x + core)


def meet(peers):
    barrier = pltpu.get_barrier_semaphore()
    for peer in peers:
        pl.semaphore_signal(barrier, inc=1, device_id=peer, device_id_type=MESH_IDS)
    pl.semaphore_wait(barrier, len(peers))


def chip_peers():
    x, core, z, y = place()
    along_z = [device(x, core, (z + k) % 4, y) for k in range(1, 4)]
    return device(1 - x, core, z, y), device(x, core, z, 1 - y), along_z


class Sender:
    def __init__(self, send, recv):
        self.send, self.recv, self.made = send, recv, []

    def start(self, src, dst, peer):
        k = len(self.made)
        copy = pltpu.make_async_remote_copy(
            src_ref=src, dst_ref=dst, send_sem=self.send.at[k], recv_sem=self.recv.at[k],
            device_id=peer, device_id_type=MESH_IDS,
        )
        copy.start()
        self.made.append(copy)
        return copy

    def close(self):
        for copy in self.made:
            copy.wait_send()


def padded_width(w):
    return -(-w // 128) * 128


def pack_piece(g, w_in, w_back, w_up, w_down, piece):
    n = w_in.shape[2]
    if g == 1:
        hid = w_up.shape[1]
        piece[:, :hid] = w_up[...].astype(LOW)
        piece[:, hid:] = w_down[...].astype(LOW)
        return
    ins, backs = GROUPS_OF[g]
    cols = [w_in[j] for j in ins] + [w_back[j].T for j in backs]
    spare = piece.shape[1] - n * len(cols)
    if spare:
        cols.append(jnp.zeros((piece.shape[0], spare), F32))
    for k in range(0, len(cols), 2):
        pair = cols[k : k + 2]
        both = pair[0] if len(pair) == 1 else jnp.concatenate(pair, axis=1)
        piece[:, n * k : n * k + both.shape[1]] = both.astype(LOW)


GROUPS_OF = {
    0: ([0, 1, 2], [0]),
    2: ([*range(7, 16), 3], []),
    3: ([], [*range(2, 11)]),
    4: ([4, 5, 6], [1]),
}


def row_of(values):
    lane = lax.broadcasted_iota(jnp.int32, (1, 128), 1)
    row = jnp.zeros((1, 128), F32)
    for j, v in enumerate(values):
        row = row + jnp.where(lane == j, v, 0.0)
    return row


def square_sum(v):
    return jnp.sum(jnp.sum(v * v, axis=1, keepdims=True), axis=0, keepdims=True)


def add_rows(target, terms, step=16):
    def body(k, carry):
        r = pl.ds(pl.multiple_of(k * step, step), step)
        total = terms[0][r, :].astype(F32)
        for t in terms[1:]:
            total = total + t[r, :].astype(F32)
        target[r, :] = total.astype(target.dtype)
        return carry

    lax.fori_loop(0, target.shape[0] // step, body, 0)


def z_peers():
    x, core, z, y = place()
    return device(x, core, z + 1 - 2 * (z % 2), y), device(x, core, (z + 2) % 4, y)


class Gather:
    def __init__(self, pieces, outs, over_x, y_first, net):
        self.pieces, self.outs, self.over_x, self.y_first, self.net = pieces, outs, over_x, y_first, net
        self.x, self.core, self.z, self.y = place()
        self.to_x, self.to_y, _ = chip_peers()
        self.to_z1, self.to_z2 = z_peers()
        near = self.z + 1 - 2 * (self.z % 2)
        self.sources = (near, (self.z + 2) % 4, (near + 2) % 4)
        self.lines, self.planes, self.corners = {}, {}, {}

    def line(self, g):
        if g in self.y_first:
            self.planes[g][0].wait_recv()
            src = dst = self.outs[g].at[0, self.z]
        else:
            src, dst = self.pieces[g], self.outs[g].at[0, self.z, self.y]
        self.lines[g] = [self.net.start(src, dst, peer) for peer in (self.to_z1, self.to_z2)]

    def relay(self, g):
        self.lines[g][1].wait_recv()
        out, far = self.outs[g], self.sources[1]
        src = out.at[0, far] if g in self.y_first else out.at[0, far, self.y]
        self.lines[g].append(self.net.start(src, src, self.to_z1))

    def own(self, g):
        z, y, out = self.z, self.y, self.outs[g]
        self.planes[g] = [self.net.start(self.pieces[g], out.at[0, z, y], self.to_y)]
        if out.shape[0] == 2:
            self.planes[g].append(self.net.start(self.pieces[g], out.at[1, z, y], self.to_x))

    def spread(self, g, k):
        if k != 2:
            self.lines[g][k - 1].wait_recv()
        out, far = self.outs[g], self.sources[k - 1]
        src = out.at[0, far, self.y]
        self.planes[g].append(self.net.start(src, src, self.to_y))
        if out.shape[0] == 2:
            self.planes[g].append(self.net.start(src, out.at[1, far, self.y], self.to_x))

    def turn(self, g):
        for c in self.planes[g]:
            c.wait_recv()
        out, y, k = self.outs[g], self.y, self.over_x[g]
        self.corners[g] = []
        if k > 0:
            self.corners[g].append(
                self.net.start(out.at[0, 0:k, 1 - y], out.at[1, 0:k, 1 - y], self.to_x)
            )
        if k < 4:
            self.corners[g].append(
                self.net.start(out.at[1, k:4, y], out.at[1, k:4, y], self.to_y)
            )

    def ready(self, g):
        if g in self.y_first:
            last = (self.lines[g][0], self.lines[g][2])
        else:
            last = self.corners[g] if self.outs[g].shape[0] == 2 else self.planes[g]
        for c in last:
            c.wait_recv()


class FourSum:
    def __init__(self, net, part, near, far_out, far_in, done):
        self.net, self.part, self.near, self.done = net, part, near, done
        self.far_out, self.far_in = far_out, far_in
        x, core, z, y = place()
        count = ROWS // 2
        self.mine = pl.ds(pl.multiple_of(core * count, count), count)
        self.theirs = pl.ds(pl.multiple_of((1 - core) * count, count), count)
        self.sibling, self.across = device(x, 1 - core, z, y), device(1 - x, core, z, y)

    def begin(self, i):
        copy = self.net.start(self.part.at[i, self.theirs, :], self.near.at[i], self.sibling)
        if i == 1:
            self.other = copy
        else:
            self.own = copy

    def cross(self):
        self.other.wait_recv()
        add_rows(self.far_out, [self.part.at[1, self.mine, :], self.near.at[1]], 64)
        self.far = self.net.start(self.far_out, self.far_in, self.across)

    def end(self):
        self.own.wait_recv()
        self.far.wait_recv()
        mine = self.done.at[self.mine, :]
        add_rows(mine, [self.part.at[0, self.mine, :], self.near.at[0], self.far_in], 64)
        self.last = self.net.start(mine, mine, self.sibling)
        self.last.wait_recv()


class Share:
    def __init__(self, net, both, first):
        self.net, self.both = net, both
        x, core, z, y = place()
        count = ROWS // 2
        self.mine = pl.ds(pl.multiple_of(first + core * count, TIME), count)
        self.sibling, self.across = device(x, 1 - core, z, y), device(1 - x, core, z, y)

    def begin(self):
        self.far = self.net.start(
            self.both.at[0, self.mine, :], self.both.at[1, self.mine, :], self.across
        )

    def pass_on(self):
        self.far.wait_recv()
        rows = self.both.at[1, self.mine, :]
        self.near = self.net.start(rows, rows, self.sibling)

    def end(self):
        self.near.wait_recv()


def matrix_of(ref, i, first, last):
    block = ref[i, :, :, :, first:last]
    return block.reshape(-1, last - first)


def forward_body(
    w_in, w_back, w_up, w_down, seg_col, seg_row, norms, side, embed, level, tokens, noises, codecs,
    g0, g1, g2, g3, g4, sq, n1_o, qkv_o, mixed_o, logs_o, resid_o, n2_o, noisy_o, first_o, conv_o,
    taps_o, resid3_o, n3_o, cq_o, ckv_o, cross_o, logs_c_o, out_o,
    p0, p1, p2, p3, p4, v0, v1, v2, v3, v4, tok, noise, codec, n1, qkv, mixed, logs, resid, n2,
    noisy, conv, taps, resid3, n3, cq, ckv, cross, logs_c, out, pad, acc, sent, got,
    part, near, far_out, far_in, summed,
    in_sem, out_sem, own_sem, send, recv,
):
    pieces, held, kept = (p0, p1, p2, p3, p4), (v0, v1, v2, v3, v4), (g0, g1, g2, g3, g4)
    n = mixed.shape[2]
    hid = w_up.shape[1]
    features = norms.shape[1]
    width = features // GROUPS
    heads = n // HD
    score_scale = HD ** (-0.5)
    net = Sender(send, recv)
    run = Gather(pieces, held, (2, 4, 0, 0, 2), (3,), net)
    share = Share(net, pad, TIME)
    total_sum = FourSum(net, part, near, far_out, far_in, summed)
    x, core, z, y = place()
    sibling = device(x, 1 - core, z, y)
    loads = [
        pltpu.make_async_copy(tokens.at[pl.ds(pl.multiple_of(x * ROWS, ROWS), ROWS), :], tok, in_sem.at[0]),
        pltpu.make_async_copy(noises.at[pl.ds(pl.multiple_of(x * ROWS, ROWS), ROWS), :], noise, in_sem.at[1]),
        pltpu.make_async_copy(codecs.at[x], codec, in_sem.at[2]),
    ]
    for c in loads:
        c.start()
    stores = []

    def store(src, dst):
        copy = pltpu.make_async_copy(src, dst, out_sem.at[len(stores)])
        copy.start()
        stores.append(copy)

    def pack(g):
        pack_piece(g, w_in, w_back, w_up, w_down, pieces[g])
        copy = pltpu.make_async_copy(pieces[g], held[g].at[0, z, y], own_sem.at[g])
        copy.start()
        return copy

    def exchange(k, total):
        sent[k] = total.astype(LOW)
        return net.start(sent.at[k], got.at[k], sibling)

    def joined(k, r):
        return sent[k, r, :].astype(F32) + got[k, r, :].astype(F32)

    local = [pack(0)]
    meet([run.to_x, run.to_y, *z_peers(), sibling])
    run.line(0)
    run.own(0)
    local.append(pack(1))
    run.line(1)
    run.own(1)
    local += [pack(2), pack(3), pack(4)]
    loads[0].wait()

    def norm_one(r):
        hat, _ = ln_stats(tok[r, :].astype(F32))
        n1[r, :] = (hat * norms[0:1, :] + norms[1:2, :]).astype(LOW)

    each_rows(norm_one)
    store(n1, n1_o)
    run.relay(0)
    run.spread(0, 1)
    run.spread(0, 2)
    run.line(2)
    run.own(3)
    run.spread(0, 3)
    run.own(2)
    sq[...] = row_of(
        [square_sum(w_in[j]) for j in range(16)] + [square_sum(w_back[j]) for j in range(11)]
        + [square_sum(w_up[...]), square_sum(w_down[...])]
    )
    run.relay(1)
    run.spread(1, 1)
    run.spread(1, 2)
    run.turn(0)
    local[0].wait()
    local[3].wait()
    run.line(3)
    run.ready(0)
    store(v0, g0)
    for i in range(2):
        qkv[i] = mm(n1[...], matrix_of(v0, i, 0, 3 * n)).astype(LOW)
    store(qkv, qkv_o)
    run.spread(1, 3)

    def self_heads(r):
        mask = seg_col[r, :] == seg_row[...]
        found = []
        for i in range(2):
            part, logs_i = softmax_heads(
                qkv[i, r, 0:n], qkv[i, :, n : 2 * n], qkv[i, :, 2 * n : 3 * n], heads, score_scale, mask
            )
            mixed[i, r, :] = part
            found += logs_i
        logs[r, :] = jnp.concatenate(found, axis=1)

    each_rows(self_heads)
    swap = exchange(
        0,
        mm_nt(mixed[0], matrix_of(v0, 0, 3 * n, 4 * n)) + mm_nt(mixed[1], matrix_of(v0, 1, 3 * n, 4 * n)),
    )
    store(mixed, mixed_o)
    store(logs, logs_o)
    run.relay(2)
    run.spread(2, 1)
    run.spread(2, 2)
    run.turn(1)
    run.own(4)
    run.line(4)
    swap.wait_recv()

    def norm_two(r):
        v = tok[r, :].astype(F32) + joined(0, r)
        resid[r, :] = v
        hat, _ = ln_stats(v)
        n2[r, :] = (hat * norms[2:3, :] + norms[3:4, :]).astype(LOW)

    each_rows(norm_two)
    store(resid, resid_o)
    store(n2, n2_o)
    run.spread(2, 3)
    run.relay(3)
    local[1].wait()
    run.ready(1)
    store(v1, g1)
    block = 256
    for i in range(2):
        for b in range(hid // block):
            pre = mm(n2[...], matrix_of(v1, i, block * b, block * (b + 1)))
            low = gelu_parts(pre)[1].astype(LOW)
            term = mm_nt(low, matrix_of(v1, i, hid + block * b, hid + block * (b + 1)))
            if i == 0 and b == 0:
                acc[...] = term
            else:
                acc[...] += term
    swap = exchange(1, acc[...])
    loads[1].wait()
    swap.wait_recv()

    def add_noise(r):
        noisy[r, :] = resid[r, :] + joined(1, r) + level[...] * noise[r, :].astype(F32)

    each_rows(add_noise)
    store(noisy, noisy_o)
    mats = group_mats(features, width)
    mats_n = group_mats(n, width)
    mean = group_average(jnp.sum(noisy[...], axis=0, keepdims=True), mats, width)
    centre = noisy[...] - mean
    var = group_average(jnp.sum(centre * centre, axis=0, keepdims=True), mats, width)
    scale = lax.rsqrt(var + NORM_EPS) * norms[4:5, :]
    for i in range(2):
        pad[i, 0:TIME, :] = jnp.zeros((TIME, features), LOW)
        pad[i, TIME + ROWS :, :] = jnp.zeros((TIME, features), LOW)

    def act(k, carry):
        r = pl.ds(pl.multiple_of(k * STEP_ROWS, STEP_ROWS), STEP_ROWS)
        v = (noisy[r, :] - mean) * scale + norms[5:6, :]
        moved = pl.ds(pl.multiple_of(TIME + k * STEP_ROWS, TIME), STEP_ROWS)
        pad[0, moved, :] = (v * jax.nn.sigmoid(v)).astype(LOW)
        return carry

    lax.fori_loop(0, ROWS // STEP_ROWS, act, 0)
    share.begin()
    run.relay(4)
    run.spread(4, 1)
    run.spread(4, 2)
    local[2].wait()
    run.ready(2)
    store(v2, g2)

    def conv_layer(i):
        q = None
        for a in range(3):
            term = mm(
                pad[i, TIME * a : TIME * a + ROWS, :], matrix_of(v2, 0, 3 * n * a, 3 * n * (a + 1))
            )
            q = term if q is None else q + term
        shift = mm(embed[i], matrix_of(v2, 0, 9 * n, 10 * n))[0:1]
        c1 = from_left(q[:, :n]) + q[:, n : 2 * n] + from_right(q[:, 2 * n :]) + shift
        conv[i] = c1
        c1 = c1 - group_average(jnp.sum(c1, axis=0, keepdims=True), mats_n, width)
        var_n = group_average(jnp.sum(c1 * c1, axis=0, keepdims=True), mats_n, width)
        v = c1 * lax.rsqrt(var_n + NORM_EPS) * side[0:1, :] + side[1:2, :]
        v = v * jax.nn.sigmoid(v)
        taps[i, 0:TIME, :] = jnp.zeros((TIME, 3 * n), LOW)
        taps[i, TIME + ROWS :, :] = jnp.zeros((TIME, 3 * n), LOW)
        taps[i, TIME : TIME + ROWS, :] = jnp.concatenate(
            [from_left(v), v, from_right(v)], axis=1
        ).astype(LOW)

    def conv_back_layer(i):
        total = None
        for a in range(3):
            term = mm_nt(
                taps[i, TIME * a : TIME * a + ROWS, :], matrix_of(v3, 0, 3 * n * a, 3 * n * (a + 1))
            )
            total = term if total is None else total + term
        part[i] = total.astype(LOW)
        total_sum.begin(i)

    conv_layer(0)
    share.pass_on()
    run.spread(4, 3)
    share.end()
    store(pad.at[:, pl.ds(TIME, ROWS), :], first_o)
    conv_layer(1)
    store(conv, conv_o)
    store(taps, taps_o)
    run.ready(3)
    store(v3, g3)
    conv_back_layer(1)
    conv_back_layer(0)
    total_sum.cross()
    local[4].wait()
    run.turn(4)
    loads[2].wait()
    run.ready(4)
    store(v4, g4)
    for i in range(2):
        ckv[i] = mm(codec[...], matrix_of(v4, i, n, 3 * n)).astype(LOW)
    store(ckv, ckv_o)
    total_sum.end()

    def norm_three(r):
        v = noisy[r, :] + summed[r, :].astype(F32)
        resid3[r, :] = v
        hat, _ = ln_stats(v)
        n3[r, :] = (hat * norms[8:9, :] + norms[9:10, :]).astype(LOW)

    each_rows(norm_three)
    store(resid3, resid3_o)
    store(n3, n3_o)
    for i in range(2):
        cq[i] = mm(n3[...], matrix_of(v4, i, 0, n)).astype(LOW)
    store(cq, cq_o)

    def cross_heads(r):
        found = []
        for i in range(2):
            part, logs_i = softmax_heads(
                cq[i, r, :], ckv[i, :, :n], ckv[i, :, n:], heads, score_scale, None
            )
            cross[i, r, :] = part
            found += logs_i
        logs_c[r, :] = jnp.concatenate(found, axis=1)

    each_rows(cross_heads)
    swap = exchange(
        2,
        mm_nt(cross[0], matrix_of(v4, 0, 3 * n, 4 * n)) + mm_nt(cross[1], matrix_of(v4, 1, 3 * n, 4 * n)),
    )
    store(cross, cross_o)
    store(logs_c, logs_c_o)
    swap.wait_recv()

    def finish_rows(r):
        out[r, :] = (resid3[r, :] + joined(2, r)).astype(LOW)

    each_rows(finish_rows)
    store(out, out_o)
    for c in stores:
        c.wait()
    net.close()


def forward_all(w_in, w_back, w_up, w_down, seg_col, seg_row, norms, side, embed, level, tokens, noises, codecs):
    n, hid = w_in.shape[2], w_up.shape[1]
    rows, features = w_in.shape[1], norms.shape[1]
    heads = 2 * n // HD
    ctok = codecs.shape[1]
    widths = [4 * n, 2 * hid, 10 * n, padded_width(9 * n), 4 * n]
    full = (ROWS, features)
    tall = ROWS + 2 * TIME
    kept = [
        (full, LOW), ((2, ROWS, 3 * n), LOW), ((2, ROWS, n), LOW), ((ROWS, heads), F32), (full, F32),
        (full, LOW), (full, F32), ((2, *full), LOW), ((2, ROWS, n), F32), ((2, tall, 3 * n), LOW),
        (full, F32), (full, LOW), ((2, ROWS, n), LOW), ((2, ctok, 2 * n), LOW), ((2, ROWS, n), LOW),
        ((ROWS, heads), F32), (full, LOW),
    ]
    groups = [(2 - (g in (2, 3)), 4, 2, rows, w) for g, w in enumerate(widths)]
    dma = pltpu.SemaphoreType.DMA
    copies = 3 * 13 + 7 + 4 + 3 + 2 + 4
    res = pl.pallas_call(
        forward_body,
        name="forward",
        in_specs=[spec_vm() for _ in range(10)] + [spec_any() for _ in range(3)],
        out_specs=[spec_any() for _ in groups] + [spec_vm()] + [spec_any() for _ in kept],
        out_shape=[jax.ShapeDtypeStruct(s, LOW) for s in groups]
        + [jax.ShapeDtypeStruct((1, 128), F32)]
        + [jax.ShapeDtypeStruct(s, t) for s, t in kept],
        scratch_shapes=[
            *[VM((rows, w), LOW) for w in widths], *[VM(s, LOW) for s in groups],
            VM(full, LOW), VM(full, LOW), VM((ctok, features), LOW), *[VM(s, t) for k, (s, t) in enumerate(kept) if k != 7],
            VM((2, tall, features), LOW), VM(full, F32), VM((3, *full), LOW), VM((3, *full), LOW),
            VM((2, *full), LOW), VM((2, ROWS // 2, features), LOW), VM((ROWS // 2, features), LOW),
            VM((ROWS // 2, features), LOW), VM(full, LOW),
            dma((3,)), dma((22,)), dma((5,)), dma((copies,)), dma((copies,)),
        ],
        compiler_params=pltpu.CompilerParams(
            collective_id=0, has_side_effects=True, vmem_limit_bytes=62 << 20
        ),
    )(w_in, w_back, w_up, w_down, seg_col, seg_row, norms, side, embed, level, tokens, noises, codecs)
    return res[:5], res[5], res[6:]


class Scatter:
    def __init__(self, net, d, over_x, bufs):
        self.net, self.d, self.k = net, d, over_x
        self.both = d.shape[0] == 2
        self.ly, self.r1, self.r2 = bufs[:3]
        if self.both:
            self.lx, self.corner = bufs[3:]
        self.x, self.core, self.z, self.y = place()
        self.to_x, self.to_y, _ = chip_peers()
        self.to_z1, self.to_z2 = z_peers()

    def raw(self):
        d, y, k, start = self.d, self.y, self.k, self.net.start
        if not self.both:
            self.first = [start(d.at[0, :, 1 - y], self.ly, self.to_y)]
            return
        self.first, self.turned = [], []
        if k > 0:
            self.turned.append(start(d.at[1, 0:k, 1 - y], self.corner.at[0:k], self.to_x))
        if k < 4:
            self.turned.append(start(d.at[1, k:4, 1 - y], self.corner.at[k:4], self.to_y))
        if k > 0:
            self.first.append(start(d.at[1, 0:k, y], self.lx.at[0:k], self.to_x))
        if k < 4:
            self.first.append(start(d.at[0, k:4, 1 - y], self.ly.at[k:4], self.to_y))

    def corners(self):
        d, y, k, start = self.d, self.y, self.k, self.net.start
        for c in self.turned:
            c.wait_recv()
        for r in range(4):
            mine = d.at[0, r, 1 - y] if r < k else d.at[1, r, y]
            add_rows(self.corner.at[r], [self.corner.at[r], mine])
        if k > 0:
            self.first.append(start(self.corner.at[0:k], self.ly.at[0:k], self.to_y))
        if k < 4:
            self.first.append(start(self.corner.at[k:4], self.lx.at[k:4], self.to_x))

    def lines(self):
        d, y, low = self.d, self.y, self.z % 2
        for c in self.first:
            c.wait_recv()
        for k in range(4):
            mine = d.at[0, k, y]
            add_rows(mine, [mine, self.ly.at[k]] + ([self.lx.at[k]] if self.both else []))
        self.ends = [
            self.net.start(d.at[0, 1 - low + 2 * h, y], self.r1.at[h], self.to_z1) for h in range(2)
        ]

    def half(self):
        d, y, z = self.d, self.y, self.z
        for h in range(2):
            self.ends[h].wait_recv()
            mine = d.at[0, z % 2 + 2 * h, y]
            add_rows(mine, [mine, self.r1.at[h]])
        self.last = self.net.start(d.at[0, (z + 2) % 4, y], self.r2, self.to_z2)

    def finish(self, target):
        self.last.wait_recv()
        add_rows(target, [self.d.at[0, self.z, self.y], self.r2])


class ScatterZ:
    def __init__(self, net, d, bufs):
        self.net, self.d, self.halves = net, d, d.shape[0]
        self.f1, self.f2, self.fy = bufs[:3]
        if self.halves == 2:
            self.pair, self.fx = bufs[3:]
        self.x, self.core, self.z, self.y = place()
        self.to_x, self.to_y, _ = chip_peers()
        self.to_z1, self.to_z2 = z_peers()

    def raw(self):
        low = self.z % 2
        self.ends = [
            self.net.start(self.d.at[:, 1 - low + 2 * h], self.f1.at[h], self.to_z1) for h in range(2)
        ]

    def half(self):
        low = self.z % 2
        for h in range(2):
            self.ends[h].wait_recv()
            for i in range(self.halves):
                for j in range(2):
                    mine = self.d.at[i, low + 2 * h, j]
                    add_rows(mine, [mine, self.f1.at[h, i, j]])
        self.next = self.net.start(self.d.at[:, (self.z + 2) % 4], self.f2, self.to_z2)

    def mid(self):
        self.next.wait_recv()
        for i in range(self.halves):
            for j in range(2):
                mine = self.d.at[i, self.z, j]
                add_rows(mine, [mine, self.f2.at[i, j]])
        self.over = self.net.start(self.d.at[:, self.z, 1 - self.y], self.fy, self.to_y)

    def turn(self):
        self.over.wait_recv()
        for i in range(2):
            add_rows(self.pair.at[i], [self.d.at[i, self.z, self.y], self.fy.at[i]])
        self.last = self.net.start(self.pair.at[1], self.fx, self.to_x)
        self.sent = [*self.ends, self.next, self.over]
        for c in self.sent:
            c.wait_send()

    def finish(self, target):
        if self.halves == 2:
            self.last.wait_recv()
            add_rows(target, [self.pair.at[0], self.fx])
        else:
            self.over.wait_recv()
            add_rows(target, [self.d.at[0, self.z, self.y], self.fy.at[0]])


class Totals:
    def __init__(self, net, values, got):
        self.net, self.values, self.got = net, values, got
        x, core, z, y = place()
        to_x, to_y, _ = chip_peers()
        self.peers = [device(x, 1 - core, z, y), to_x, to_y, *z_peers()]

    def start(self, k):
        self.copy = self.net.start(self.values.at[k], self.got.at[k], self.peers[k])

    def step(self, k):
        self.copy.wait_recv()
        self.values[k + 1] = self.values[k] + self.got[k]
        if k < 4:
            self.start(k + 1)


def backward_body(
    seg_col, seg_row, norms, side, embed_rows, sq, tokens, cots, codecs,
    g0, g1, g2, g3, g4, n1_h, qkv_h, mixed_h, logs_h, resid_h, n2_h, noisy_h, first_h, conv_h, taps_h,
    resid3_h, n3_h, cq_h, ckv_h, cross_h, logs_c_h, out_h,
    s0, s1, s2, s3, s4, grad_x, other_x, other_out, rows_o,
    d_c, d_t, d_o, d_m, wv, cot, codec, cq, ckv, cross, gm, logs, resid, nrm, grad, pad, taps, tapsg,
    conv, first, hb, hb2, acc, sent, got, part, near, far_out, far_in, summed,
    f1_c, f2_c, fy_c, pair_c, fx_c, ly_t, r1_t, r2_t, f1_o, f2_o, fy_o,
    ly_m, r1_m, r2_m, lx_m, co_m, ly_a, r1_a, r2_a, lx_a, co_a, values, values_in,
    stage, gsum, load_sem, out_sem, send, recv,
):
    n = cq.shape[2]
    features = norms.shape[1]
    width = features // GROUPS
    heads = n // HD
    hid = g1.shape[2] // 2
    block = d_m.shape[5] // 2
    ctok = codec.shape[0]
    score_scale = HD ** (-0.5)
    x, core, z, y = place()
    to_x, to_y, _ = chip_peers()
    sibling = device(x, 1 - core, z, y)
    net = Sender(send, recv)
    loads = []

    def load(src, dst):
        copy = pltpu.make_async_copy(src, dst, load_sem.at[len(loads)])
        copy.start()
        loads.append(copy)
        return copy

    def weights(ref, i):
        w = ref.shape[2]
        return load(ref.at[i], wv.at[i, :, pl.ds(0, w)])

    own = pl.ds(pl.multiple_of(x * ROWS, ROWS), ROWS)
    half = pl.ds(pl.multiple_of(core * (ROWS // 2), ROWS // 2), ROWS // 2)
    ready = [
        load(cots.at[own, :], cot), load(cross_h, cross), load(g4.at[0], wv.at[0, :, pl.ds(0, 4 * n)]),
        load(g4.at[1], wv.at[1, :, pl.ds(0, 4 * n)]), load(cq_h, cq), load(ckv_h, ckv),
        load(logs_c_h, logs), load(n3_h, nrm), load(codecs.at[x], codec),
    ]
    later = [load(resid3_h, resid), load(taps_h, taps), load(conv_h, conv), load(first_h, first)]
    meet([to_x, to_y, *z_peers(), sibling])
    out_far = net.start(out_h.at[half, :], other_out.at[half, :], to_x)
    sends = {}
    cro = ScatterZ(net, d_c, (f1_c, f2_c, fy_c, pair_c, fx_c))
    two = Scatter(net, d_t, 0, (ly_t, r1_t, r2_t))
    one = ScatterZ(net, d_o, (f1_o, f2_o, fy_o))
    mlp = [
        Scatter(net, d_m.at[q], 3, (ly_m.at[q], r1_m.at[q], r2_m.at[q], lx_m.at[q], co_m.at[q]))
        for q in range(hid // block)
    ]
    attn = Scatter(net, d_c, 2, (ly_a, r1_a, r2_a, lx_a, co_a))
    rows = values.at[0]
    totals = Totals(net, values, values_in)
    share = Share(net, pad, TIME)
    total_sum = FourSum(net, part, near, far_out, far_in, summed)

    def exchange(k, total):
        if k >= 2:
            sends[k - 2].wait_send()
        sent[k % 2] = total.astype(LOW)
        sends[k] = net.start(sent.at[k % 2], got.at[k % 2], sibling)

    def joined(k, r):
        return sent[k % 2, r, :].astype(F32) + got[k % 2, r, :].astype(F32)

    def put(ref, i, first, value):
        w = value.shape[1]
        ref[i, :, :, :, first : first + w] = value.astype(LOW).reshape(4, 2, -1, w)

    values[0] = jnp.zeros(values.shape[1:], F32)
    rows[10:11, 0:128] = sq[...]
    gsum[...] = jnp.zeros(gsum.shape, F32)
    for c in ready:
        c.wait()
    for i in (1, 0):
        gm[i] = mm(cot[...], wv[i, :, 3 * n : 4 * n]).astype(LOW)
    acc_kv = acc.at[0:ctok, :]
    acc_kv[...] = jnp.zeros((ctok, 4 * n), F32)

    def cross_heads(r):
        for i in range(2):
            rows_logs = [logs[r, heads * i + h : heads * i + h + 1] for h in range(heads)]
            gq, gk, gv = softmax_heads_back(
                cq[i, r, :], ckv[i, :, :n], ckv[i, :, n:], gm[i, r, :], rows_logs, heads, score_scale, None
            )
            cq[i, r, :] = gq.astype(LOW)
            acc_kv[:, 2 * n * i : 2 * n * (i + 1)] += jnp.concatenate([gk, gv], axis=1)

    each_rows(cross_heads)
    exchange(0, mm_nt(cq[1], wv[1, :, :n]) + mm_nt(cq[0], wv[0, :, :n]))
    for i in (1, 0):
        both = acc_kv[:, 2 * n * i : 2 * n * (i + 1)]
        low = jnp.concatenate([both[:, :n] * score_scale, both[:, n:]], axis=1).astype(LOW)
        put(d_c, i, 3 * n, mm_tn(cot[...], cross[i]))
        put(d_c, i, 0, mm_tn(nrm[...], cq[i]))
        put(d_c, i, n, mm_tn(codec[...], low))
    cro.raw()
    two_w = load(g3.at[0], wv.at[0, :, pl.ds(0, g3.shape[2])])
    one_w = load(g2.at[0], wv.at[1, :, pl.ds(0, g2.shape[2])])
    for i in range(2):
        pad[i, 0:TIME, :] = jnp.zeros((TIME, features), LOW)
        pad[i, TIME + ROWS :, :] = jnp.zeros((TIME, features), LOW)
    low_grad = pad.at[0, TIME : TIME + ROWS, :]
    other_grad = pad.at[1, TIME : TIME + ROWS, :]
    for c in later:
        c.wait()
    sends[0].wait_recv()

    def pull_three(r):
        back, gain, shift = ln_back(resid[r, :], norms[8:9, :], joined(0, r))
        v = cot[r, :].astype(F32) + back
        grad[r, :] = v
        low_grad[r, :] = v.astype(LOW)
        rows[8:9, :] += gain
        rows[9:10, :] += shift

    each_rows(pull_three)
    share.begin()
    tok_load = load(tokens.at[own, :], cot)
    noisy_load = load(noisy_h, resid)
    n2_load = load(n2_h, nrm)
    mats_n = group_mats(n, width)
    gn_rows = [None, None]
    two_w.wait()

    def conv_pull(i):
        q = None
        for a in range(3):
            term = mm(
                pad[i, TIME * (2 - a) : TIME * (2 - a) + ROWS, :], wv[0, :, 3 * n * a : 3 * n * (a + 1)]
            )
            q = term if q is None else q + term
        g = from_right(q[:, :n]) + q[:, n : 2 * n] + from_left(q[:, 2 * n :])
        c1 = conv[i]
        c1 = c1 - group_average(jnp.sum(c1, axis=0, keepdims=True), mats_n, width)
        var_n = group_average(jnp.sum(c1 * c1, axis=0, keepdims=True), mats_n, width)
        scale = lax.rsqrt(var_n + NORM_EPS)
        hat = c1 * scale
        gain = side[0:1, :]
        pre = hat * gain + side[1:2, :]
        gate = jax.nn.sigmoid(pre)
        g = g * gate * (1.0 + pre * (1.0 - gate))
        d_gain = jnp.sum(g * hat, axis=0, keepdims=True)
        d_shift = jnp.sum(g, axis=0, keepdims=True)
        gn_rows[i] = jnp.concatenate([d_gain, d_shift], axis=0)
        back = scale * (
            g * gain
            - group_average(d_shift * gain, mats_n, width)
            - hat * group_average(d_gain * gain, mats_n, width)
        )
        back = back.astype(LOW).astype(F32)
        gsum[i : i + 1, :] = jnp.sum(back, axis=0, keepdims=True)
        tapsg[i, 0:TIME, :] = jnp.zeros((TIME, 3 * n), LOW)
        tapsg[i, TIME + ROWS :, :] = jnp.zeros((TIME, 3 * n), LOW)
        tapsg[i, TIME : TIME + ROWS, :] = jnp.concatenate(
            [from_right(back), back, from_left(back)], axis=1
        ).astype(LOW)

    def first_pull(i):
        total = None
        for a in range(3):
            term = mm_nt(
                tapsg[i, TIME * (2 - a) : TIME * (2 - a) + ROWS, :], wv[1, :, 3 * n * a : 3 * n * (a + 1)]
            )
            total = term if total is None else total + term
        part[i] = total.astype(LOW)
        total_sum.begin(i)

    conv_pull(0)
    out_far.wait_recv()
    out_near = net.start(other_out.at[half, :], other_out.at[half, :], sibling)
    share.pass_on()
    share.end()
    conv_pull(1)
    one_w.wait()
    first_pull(1)
    first_pull(0)
    cro.half()
    total_sum.cross()
    for a in range(3):
        put(
            d_t, 0, 3 * n * a,
            mm_tn(low_grad[...], taps[0, TIME * a : TIME * a + ROWS, :])
            + mm_tn(other_grad[...], taps[1, TIME * a : TIME * a + ROWS, :]),
        )
    d_t[:, :, :, :, 9 * n :] = jnp.zeros((*d_t.shape[:4], d_t.shape[4] - 9 * n), LOW)
    two.raw()
    gn_both = gn_rows[0] + gn_rows[1]
    rows[6:8, :] = jnp.concatenate(
        [jnp.where(2 * x + core == s, gn_both, 0.0) for s in range(4)], axis=1
    )
    for a in range(3):
        window = pl.ds(TIME * (2 - a), ROWS)
        put(
            d_o, 0, 3 * n * a,
            mm_tn(first[0], tapsg[0, window, :]) + mm_tn(first[1], tapsg[1, window, :]),
        )
    put(
        d_o, 0, 9 * n,
        lax.dot_general(
            embed_rows[...], gsum[...], (((0,), (0,)), ((), ())), precision=HIGHEST_PRECISION,
            preferred_element_type=F32,
        ),
    )
    mlp_w = [weights(g1, i) for i in range(2)]
    total_sum.end()
    one.raw()

    noisy_load.wait()
    mats = group_mats(features, width)
    mean = group_average(jnp.sum(resid[...], axis=0, keepdims=True), mats, width)
    centre = resid[...] - mean
    var = group_average(jnp.sum(centre * centre, axis=0, keepdims=True), mats, width)
    scale = lax.rsqrt(var + NORM_EPS)
    gain, shift = norms[4:5, :], norms[5:6, :]

    def through_silu(r):
        hat = (resid[r, :] - mean) * scale
        pre = hat * gain + shift
        gate = jax.nn.sigmoid(pre)
        g = summed[r, :].astype(F32)
        g = g * gate * (1.0 + pre * (1.0 - gate))
        acc[r, :] = g
        rows[4:5, :] += jnp.sum(g * hat, axis=0, keepdims=True)
        rows[5:6, :] += jnp.sum(g, axis=0, keepdims=True)

    each_rows(through_silu)
    mean_shift = group_average(rows[5:6, :] * gain, mats, width)
    mean_gain = group_average(rows[4:5, :] * gain, mats, width)

    def pull_two(r):
        hat = (resid[r, :] - mean) * scale
        v = grad[r, :] + scale * (acc[r, :] * gain - mean_shift - hat * mean_gain)
        grad[r, :] = v
        low_grad[r, :] = v.astype(LOW)

    share.far.wait_send()
    each_rows(pull_two)
    resid_load = load(resid_h, resid)
    n2_load.wait()
    for c in mlp_w:
        c.wait()
    for q, group in enumerate(mlp):
        up, down = block * q, hid + block * q
        for i in (1, 0):
            pre = mm(nrm[...], wv[i, :, up : up + block])
            t, hidden = gelu_parts(pre)
            slope = gelu_slope(pre, t)
            hb[i] = hidden.astype(LOW)
            hb2[i] = (mm(low_grad[...], wv[i, :, down : down + block]) * slope).astype(LOW)
            term = mm_nt(hb2[i], wv[i, :, up : up + block])
            if q == 0 and i == 1:
                acc[...] = term
            else:
                acc[...] += term
        if q == len(mlp) - 1:
            exchange(1, acc[...])
        for i in (1, 0):
            put(d_m.at[q], i, block, mm_tn(low_grad[...], hb[i]))
            put(d_m.at[q], i, 0, mm_tn(nrm[...], hb2[i]))
        group.raw()
        if q == 1:
            cro.mid()
    attn_w = [weights(g0, i) for i in range(2)]
    tail_loads = [
        load(n1_h, nrm), load(qkv_h, tapsg.at[:, pl.ds(0, ROWS), :]), load(mixed_h, cross), load(logs_h, logs),
    ]
    resid_load.wait()
    sends[1].wait_recv()

    def pull_one(r):
        back, g_gain, g_shift = ln_back(resid[r, :], norms[2:3, :], joined(1, r))
        v = grad[r, :] + back
        grad[r, :] = v
        low_grad[r, :] = v.astype(LOW)
        rows[2:3, :] += g_gain
        rows[3:4, :] += g_shift

    each_rows(pull_one)
    for c in (*attn_w, *tail_loads):
        c.wait()
    for i in range(2):
        gm[i] = mm(low_grad[...], wv[i, :, 3 * n : 4 * n]).astype(LOW)
    acc[...] = jnp.zeros(acc.shape, F32)

    def self_heads(r):
        mask = seg_col[r, :] == seg_row[...]
        for i in range(2):
            rows_logs = [logs[r, heads * i + h : heads * i + h + 1] for h in range(heads)]
            gq, gk, gv = softmax_heads_back(
                tapsg[i, r, :n], tapsg[i, 0:ROWS, n : 2 * n], tapsg[i, 0:ROWS, 2 * n :], gm[i, r, :],
                rows_logs, heads, score_scale, mask,
            )
            taps[i, r, :n] = gq.astype(LOW)
            acc[:, 2 * n * i : 2 * n * (i + 1)] += jnp.concatenate([gk, gv], axis=1)

    each_rows(self_heads)
    one.half()
    cro.turn()
    mlp[0].corners()
    for i in (1, 0):
        both = acc[:, 2 * n * i : 2 * n * (i + 1)]
        taps[i, 0:ROWS, n:] = jnp.concatenate([both[:, :n] * score_scale, both[:, n:]], axis=1).astype(LOW)
        put(d_c, i, 3 * n, mm_tn(low_grad[...], cross[i]))
        put(d_c, i, 0, mm_tn(nrm[...], taps[i, 0:ROWS, :]))
    attn.raw()
    exchange(
        2, mm_nt(taps[1, 0:ROWS, :], wv[1, :, : 3 * n]) + mm_nt(taps[0, 0:ROWS, :], wv[0, :, : 3 * n])
    )
    two.lines()
    tok_load.wait()
    sends[2].wait_recv()

    def pull_zero(r):
        back, g_gain, g_shift = ln_back(cot[r, :].astype(F32), norms[0:1, :], joined(2, r))
        low_grad[r, :] = (grad[r, :] + back).astype(LOW)
        rows[0:1, :] += g_gain
        rows[1:2, :] += g_shift

    each_rows(pull_zero)
    store_x = pltpu.make_async_copy(low_grad, grad_x, out_sem.at[5])
    store_x.start()
    middle = pl.ds(pl.multiple_of(TIME + core * (ROWS // 2), TIME), ROWS // 2)
    x_far = net.start(pad.at[0, middle, :], other_x.at[half, :], to_x)
    rows[0:6, :] = jnp.where(core == 0, rows[0:6, :], 0.0)
    rows[8:10, :] = jnp.where(core == 0, rows[8:10, :], 0.0)
    totals.start(0)

    def deliver(group, k, out):
        w = out.shape[1]
        part = stage.at[:, pl.ds(0, w)]
        group.finish(part)
        copy = pltpu.make_async_copy(part, out, out_sem.at[k])
        copy.start()
        copy.wait()

    mlp[1].corners()
    mlp[0].lines()
    totals.step(0)
    mlp[2].corners()
    deliver(cro, 0, s4)
    totals.step(1)
    mlp[0].half()
    one.mid()
    mlp[1].lines()
    totals.step(2)
    deliver(mlp[0], 1, s1.at[0])
    mlp[2].lines()
    two.half()
    attn.corners()
    totals.step(3)
    x_far.wait_recv()
    x_near = net.start(other_x.at[half, :], other_x.at[half, :], sibling)
    mlp[1].half()
    deliver(one, 2, s2)
    attn.lines()
    mlp[2].half()
    totals.step(4)
    rows_o[...] = values[5]
    deliver(mlp[1], 3, s1.at[1])
    deliver(mlp[2], 4, s1.at[2])
    attn.half()
    deliver(two, 6, s3)
    deliver(attn, 7, s0)
    out_near.wait_recv()
    x_near.wait_recv()
    store_x.wait()
    wait_sends(net, [sends[0], share.far, *cro.sent])


def wait_sends(net, done):
    for copy in net.made:
        if all(copy is not d for d in done):
            copy.wait_send()


def backward_all(seg_col, seg_row, norms, side, embed_rows, sq, tokens, cots, codecs, gathered, kept):
    features = norms.shape[1]
    n = side.shape[1]
    rows = gathered[0].shape[3]
    widths = [g.shape[4] for g in gathered]
    hid = widths[1] // 2
    heads = 2 * n // HD
    ctok = codecs.shape[1]
    full = (ROWS, features)
    tall = ROWS + 2 * TIME
    ins = [
        seg_col, seg_row, norms, side, embed_rows, sq, tokens, cots, codecs,
        *[g.reshape(g.shape[0], features, -1) for g in gathered], *kept,
    ]
    dma = pltpu.SemaphoreType.DMA

    block = 256
    parts = hid // block

    def pieces(width, *counts):
        return [VM((*(k if isinstance(k, tuple) else (k,)), rows, width), LOW) for k in counts]

    copies = 2 + 3 + 2 + 2 + 4 + 5 + 5 + 4 + 4 + parts * 9 + 9
    res = pl.pallas_call(
        backward_body,
        name="backward",
        in_specs=[spec_vm() for _ in range(6)] + [spec_any() for _ in ins[6:]],
        out_specs=[spec_any() for _ in range(8)] + [spec_vm()],
        out_shape=[
            jax.ShapeDtypeStruct((parts, rows, 2 * block) if g == 1 else (rows, w), F32)
            for g, w in enumerate(widths)
        ]
        + [jax.ShapeDtypeStruct(full, LOW)] * 3
        + [jax.ShapeDtypeStruct((16, features), F32)],
        scratch_shapes=[
            VM((2, 4, 2, rows, 4 * n), LOW), VM((1, 4, 2, rows, widths[3]), LOW),
            VM((1, 4, 2, rows, 10 * n), LOW), VM((parts, 2, 4, 2, rows, 2 * block), LOW),
            VM((2, features, 10 * n), LOW), VM(full, LOW), VM((ctok, features), LOW),
            VM((2, ROWS, n), LOW), VM((2, ctok, 2 * n), LOW), VM((2, ROWS, n), LOW), VM((2, ROWS, n), LOW),
            VM((ROWS, heads), F32), VM(full, F32), VM(full, LOW), VM(full, F32),
            VM((2, tall, features), LOW), VM((2, tall, 3 * n), LOW), VM((2, tall, 3 * n), LOW),
            VM((2, ROWS, n), F32), VM((2, *full), LOW), VM((2, ROWS, 256), LOW), VM((2, ROWS, 256), LOW), VM(full, F32),
            VM((2, *full), LOW), VM((2, *full), LOW), VM((2, *full), LOW),
            VM((2, ROWS // 2, features), LOW), VM((ROWS // 2, features), LOW),
            VM((ROWS // 2, features), LOW), VM(full, LOW),
            *pieces(4 * n, (2, 2, 2), (2, 2), 2, 2), VM((rows, 4 * n), LOW),
            *pieces(widths[3], 4, 2), VM((rows, widths[3]), LOW),
            *pieces(10 * n, (2, 1, 2), (1, 2), 1),
            *pieces(2 * block, (parts, 4), (parts, 2), parts, (parts, 4), (parts, 4)),
            *pieces(4 * n, 4, 2), VM((rows, 4 * n), LOW), *pieces(4 * n, 4, 4),
            VM((6, 16, features), F32), VM((5, 16, features), F32),
            VM((rows, 10 * n), F32), VM((8, n), F32),
            dma((30,)), dma((8,)), dma((copies,)), dma((copies,)),
        ],
        compiler_params=pltpu.CompilerParams(
            collective_id=1, has_side_effects=True, vmem_limit_bytes=64 << 20
        ),
    )(*ins)
    return res[:5], res[5], res[6], res[7], res[8]


def adam_rows(w, g, m, v, decay_rate):
    m_new = MOMENT_DECAY * m + (1.0 - MOMENT_DECAY) * g
    v_new = MOMENT_DECAY * v + (1.0 - MOMENT_DECAY) * g * g
    correct = 1.0 - MOMENT_DECAY**STEP
    update = m_new / correct / (jnp.sqrt(v_new / correct) + ADAM_EPS) + decay_rate * w
    return m_new, v_new, update


def moments_body(*refs):
    sums, refs = refs[:5], refs[5:]
    w_in, w_back, w_up, w_down, m_in, m_back, m_up, m_down, v_in, v_back, v_up, v_down = refs[:12]
    nm_in, nm_back, nm_up, nm_down, nv_in, nv_back, nv_up, nv_down = refs[12:20]
    u_in, u_back, u_up, u_down, usq = refs[20:]
    n = w_in.shape[2]
    squares = [None] * 29

    def place_in(j, g):
        m, v, u = adam_rows(w_in[j], g, m_in[j], v_in[j], WEIGHT_DECAY)
        nm_in[j], nv_in[j], u_in[j] = m, v, u
        squares[j] = square_sum(u)

    def place_back(j, g):
        m, v, u = adam_rows(w_back[j], g.T, m_back[j], v_back[j], WEIGHT_DECAY)
        nm_back[j], nv_back[j], u_back[j] = m, v, u
        squares[16 + j] = square_sum(u)

    for g, (ins, backs) in GROUPS_OF.items():
        for k, j in enumerate(ins):
            place_in(j, sums[g][:, n * k : n * (k + 1)])
        for k, j in enumerate(backs, len(ins)):
            place_back(j, sums[g][:, n * k : n * (k + 1)])
    block = sums[1].shape[2] // 2
    up_sq, down_sq = [], []
    for q in range(w_up.shape[1] // block):
        cols = slice(block * q, block * (q + 1))
        m, v, u = adam_rows(w_up[:, cols], sums[1][q, :, :block], m_up[:, cols], v_up[:, cols], WEIGHT_DECAY)
        nm_up[:, cols], nv_up[:, cols], u_up[:, cols] = m, v, u
        up_sq.append(square_sum(u))
        m, v, u = adam_rows(
            w_down[:, cols], sums[1][q, :, block:], m_down[:, cols], v_down[:, cols], WEIGHT_DECAY
        )
        nm_down[:, cols], nv_down[:, cols], u_down[:, cols] = m, v, u
        down_sq.append(square_sum(u))
    squares[27] = sum(up_sq)
    squares[28] = sum(down_sq)
    usq[...] = row_of(squares)


def totals_body(usq, out, ring, ring_b, send, recv):
    mp, dp = lax.axis_index("mp"), lax.axis_index("dp")
    dp_peers = [((dp + k) % 8, mp) for k in range(1, 8)]
    mp_peers = [(dp, (mp + k) % 4) for k in range(1, 4)]
    ring[dp] = jnp.broadcast_to(usq[...], ring.shape[1:])
    meet(dp_peers + mp_peers)
    net = Sender(send, recv)
    copies = [net.start(ring.at[dp], ring.at[dp], p) for p in dp_peers]
    for c in copies:
        c.wait_recv()
    total = ring[0]
    for k in range(1, 8):
        total = total + ring[k]
    ring_b[mp] = total
    copies = [net.start(ring_b.at[mp], ring_b.at[mp], p) for p in mp_peers]
    for c in copies:
        c.wait_recv()
    out[...] = ring_b[0] + ring_b[1] + ring_b[2] + ring_b[3]
    net.close()


def apply_body(total, sums, w_in, w_back, w_up, w_down, u_in, u_back, u_up, u_down, norms, norm_m, norm_v, *outs):
    nw_in, nw_back, nw_up, nw_down, new_norm, new_nm, new_nv, lens = outs
    both = jnp.sqrt(jnp.concatenate([total[10:11, 0:128], sums[0:1, :]], axis=0))
    lens[...] = both[:, 0:29]
    trust = LEARN_RATE * (both[0:1, :] / jnp.where(both[1:2, :] == 0.0, 1.0, both[1:2, :]))
    lane = lax.broadcasted_iota(jnp.int32, (1, 128), 1)

    def trust_of(j):
        return jnp.sum(jnp.where(lane == j, trust, 0.0), axis=1, keepdims=True)

    for j in range(16):
        nw_in[j] = w_in[j] - trust_of(j) * u_in[j]
    for j in range(11):
        nw_back[j] = w_back[j] - trust_of(16 + j) * u_back[j]
    nw_up[...] = w_up[...] - trust_of(27) * u_up[...]
    nw_down[...] = w_down[...] - trust_of(28) * u_down[...]
    m, v, u = adam_rows(norms[...], total[0:10, :], norm_m[...], norm_v[...], 0.0)
    w = norms[...]
    row_trust = jnp.sqrt(jnp.sum(w * w, axis=1, keepdims=True)) / jnp.sqrt(
        jnp.sum(u * u, axis=1, keepdims=True)
    )
    new_norm[...] = w - LEARN_RATE * row_trust * u
    new_nm[...] = m
    new_nv[...] = v


def lamb_all(sums, rows, masters, moments, squares, norms, norm_m, norm_v):
    shapes = [(v.shape, F32) for v in masters]
    *mvu, usq = run_kernel(
        moments_body, "lamb_moments", [*sums, *masters, *moments, *squares],
        [*shapes, *shapes, *shapes, ((1, 128), F32)], [],
    )
    dma = pltpu.SemaphoreType.DMA
    usq_sum = pl.pallas_call(
        totals_body,
        name="norm_totals",
        in_specs=[spec_vm()],
        out_specs=spec_vm(),
        out_shape=jax.ShapeDtypeStruct((8, 128), F32),
        scratch_shapes=[VM((8, 8, 128), F32), VM((4, 8, 128), F32), dma((10,)), dma((10,))],
        compiler_params=pltpu.CompilerParams(collective_id=2, has_side_effects=True),
    )(usq)
    *weights, new_norm, new_nm, new_nv, lens = run_kernel(
        apply_body, "lamb_apply", [rows, usq_sum, *masters, *mvu[8:], norms, norm_m, norm_v],
        [*shapes, *[(norms.shape, F32)] * 3, ((2, 29), F32)], [],
    )
    return (*weights, *mvu[:8], new_norm, new_nm, new_nv, lens)


def fast_device(
    tokens,
    noise_field,
    codec_tokens,
    timesteps,
    segments,
    cotangent,
    w_in,
    w_back,
    w_up,
    w_down,
    m_in,
    m_back,
    m_up,
    m_down,
    v_in,
    v_back,
    v_up,
    v_down,
    norm_params,
    norm_m,
    norm_v,
):
    features = tokens.shape[1]
    n = w_in.shape[2]
    mp = lax.axis_index("mp")
    dp = lax.axis_index("dp")
    x, core, z, y = mp // 2, mp % 2, dp // 2, dp % 2

    steps = by_parity(x, timesteps[0], timesteps[1], 0)
    seg = pick(segments, x, 0)
    seg_col, seg_row = seg[:, None], seg[None, :]
    noise_level = jnp.sqrt((steps[0].astype(F32) + 1.0) / TSTEPS).reshape(1, 1)
    embed = jax.nn.silu(time_embedding(steps, features)).astype(LOW)
    embed_rows = jnp.broadcast_to(embed[:, None], (2, 8, features))
    embed_eight = jnp.pad(embed.astype(F32), ((0, 6), (0, 0)))
    side = lax.dynamic_slice(norm_params, (6, (2 * x + core) * n), (2, n))
    norms = norm_params

    gathered, weight_sq, kept = forward_all(
        w_in, w_back, w_up, w_down.T, seg_col, seg_row, norms, side, embed_rows, noise_level,
        tokens, noise_field, codec_tokens,
    )
    sums, own_x, other_x, other_out, rows = backward_all(
        seg_col, seg_row, norms, side, embed_eight, weight_sq, tokens, cotangent, codec_tokens, gathered, kept
    )
    out_rows = by_parity(x, kept[-1], other_out, 0).reshape(-1, features)
    grad_rows = by_parity(x, own_x, other_x, 0).reshape(-1, features).astype(F32)
    stepped = lamb_all(
        sums, rows, (w_in, w_back, w_up, w_down.T), (m_in, m_back, m_up, m_down.T),
        (v_in, v_back, v_up, v_down.T), norm_params, norm_m, norm_v,
    )
    stepped = [v.T if k in (3, 7, 11) else v for k, v in enumerate(stepped)]
    return (out_rows, grad_rows, *stepped)


def solution(mesh):
    per_device = fast_device if dict(mesh.shape) == {"dp": 8, "mp": 4} else generic_device
    placed = (
        P("dp", None),
        P("dp", None),
        P("dp", None, None),
        P("dp"),
        P("dp", None),
        P("dp", None),
        P(None, "dp", "mp"),
        P(None, "mp", "dp"),
        P("dp", "mp"),
        P("mp", "dp"),
        P(None, "dp", "mp"),
        P(None, "mp", "dp"),
        P("dp", "mp"),
        P("mp", "dp"),
        P(None, "dp", "mp"),
        P(None, "mp", "dp"),
        P("dp", "mp"),
        P("mp", "dp"),
        P(),
        P(),
        P(),
    )
    return jax.shard_map(
        per_device,
        mesh=mesh,
        in_specs=placed,
        out_specs=(
            P("dp", None),
            P("dp", None),
            P(None, "dp", "mp"),
            P(None, "mp", "dp"),
            P("dp", "mp"),
            P("mp", "dp"),
            P(None, "dp", "mp"),
            P(None, "mp", "dp"),
            P("dp", "mp"),
            P("mp", "dp"),
            P(None, "dp", "mp"),
            P(None, "mp", "dp"),
            P("dp", "mp"),
            P("mp", "dp"),
            P(),
            P(),
            P(),
            P(),
        ),
        check_vma=False,
    )
```

profile of v0, /device:TPU:0, one launch (start us, length us, event | category | flops | bytes accessed | tf_op | source)
XLA Modules:
  0.0 411.3 jit_solution(15945432437091093911)
XLA Ops:
  0.7 1.3 fusion.1
  4.6 0.1 add_convert_fusion
  4.7 1.4 constant_dynamic-slice_fusion.side
  6.1 1.3 constant_dynamic-slice_fusion.1.seg_row
  7.3 0.7 fusion.2
  8.0 0.1 multiply_sine_fusion
  8.2 0.6 pad_convert_fusion.embed_rows
  8.8 0.6 broadcast_in_dim.5.embed
  9.4 0.9 copy.39.seg_col
  10.3 176.4 %forward.1 = (bf16[2,4,2,96,768]{4,3,2,1,0:T(8,128)(2,1)}, bf16[2,4,2,96,1536]{4,3,2,1,0:T(8,128)(2,1)}, bf16[1,4,2,96,1920]{4,3,2,1,0:T(8,128)(2,1)}, bf16[1,4,...) custom-call(f32[16,96,192]{2,1,0:T(8,128)} %w_in.3, ...), custom_call_target="tpu_custom_call" | custom-call | tf_op jit(solution)/shard_map/forward/pallas_call | solution.py:1108
  186.7 192.4 %backward.1 = (f32[96,768]{1,0:T(8,128)}, f32[3,96,512]{2,1,0:T(8,128)}, f32[96,1920]{1,0:T(8,128)}, f32[96,1792]{1,0:T(8,128)}, f32[96,768]{1,0:T(8,128)}, /*in...) custom-call(s32[512,1]{1,0:T(8,128)} %copy.39.seg_col, ...), custom_call_target="tpu_custom_call" | custom-call | tf_op jit(solution)/shard_map/backward/pallas_call | solution.py:1664
  379.1 2.1 select_bitcast_fusion.1
  381.2 0.1 pad_maximum_fusion.1
  381.4 2.0 bitcast_convert_fusion
  383.4 1.3 pad_maximum_fusion
  384.6 11.7 %lamb_moments.1 = (f32[16,96,192]{2,1,0:T(8,128)}, f32[11,192,96]{2,1,0:T(8,128)}, f32[96,768]{1,0:T(8,128)}, f32[96,768]{1,0:T(8,128)}, f32[16,96,192]{2,1,0:T(...) custom-call(f32[96,768]{1,0:T(8,128)} %get-tuple-element.98.refs_0_,, ...), custom_call_target="tpu_custom_call" | custom-call | bytes 18088448 | tf_op jit(solution)/shard_map/lamb_moments/pallas_call | solution.py:495
  396.3 9.7 %norm_totals.1.sums = f32[8,128]{1,0:T(8,128)} custom-call(f32[1,128]{1,0:T(1,128)} %get-tuple-element.103.usq), custom_call_target="tpu_custom_call" | custom-call | tf_op jit(solution)/shard_map/norm_totals/pallas_call | solution.py:1804
  406.0 4.8 %lamb_apply.1 = (f32[16,96,192]{2,1,0:T(8,128)}, f32[11,192,96]{2,1,0:T(8,128)}, f32[96,768]{1,0:T(8,128)}, f32[96,768]{1,0:T(8,128)}, f32[10,768]{1,0:T(8,128)}...) custom-call(f32[16,768]{1,0:T(8,128)} %get-tuple-element.97.total, f32[8,128]{1,0:T(8,128)} %norm_totals.1.sums, ...), custom_call_target="tpu_custom_call" | custom-call | bytes 7979240 | tf_op jit(solution)/shard_map/lamb_apply/pallas_call | solution.py:495
  (2 shorter events, 0.0 us)
where the time goes:
time: 418 us; the launch traced here: 411 us
  Pallas kernels  395 us (94%)
  other arithmetic  6.33 us (2%)
  local copies, waits for them, and re-layouts  6.1 us (1%)
    pallas_call x1, Pallas kernels, backward_all(): pl.pallas_call(backward_body, name='backward', in_specs=[spec_vm() for _...  192 us
    pallas_call x1, Pallas kernels, forward_all(): pl.pallas_call(forward_body, name='forward', in_specs=[spec_vm() for _ in...  176 us
    pallas_call x2, Pallas kernels, run_kernel(): pl.pallas_call(body, name=name, in_specs=in_specs, out_specs=[spec_vm() f...  16.5 us
    pallas_call x1, Pallas kernels, lamb_all(): pl.pallas_call(totals_body, name='norm_totals', in_specs=[spec_vm()], out...  9.67 us

commit v1 on v0

--- a/solution.py
+++ b/solution.py
@@ -620,6 +620,16 @@
     return device(1 - x, core, z, y), device(x, core, z, 1 - y), along_z
 
 
+def own_segments(segments, x, seg_col):
+    row = jnp.where(x == 0, segments[0:1, :], segments[1:2, :]).astype(F32)
+    seg_col[...] = jnp.broadcast_to(row, (8, row.shape[1])).T[:, 0:1]
+    return row
+
+
+def own_channels(norms, which, n):
+    return sum(jnp.where(which == s, norms[6:8, n * s : n * (s + 1)], 0.0) for s in range(4))
+
+
 class Sender:
     def __init__(self, send, recv):
         self.send, self.recv, self.made = send, recv, []
@@ -634,9 +644,51 @@
         self.made.append(copy)
         return copy
 
+    def reserve(self, count, item):
+        base = len(self.made)
+        self.made += [item] + [None] * (count - 1)
+        return base
+
     def close(self):
         for copy in self.made:
-            copy.wait_send()
+            if copy is not None:
+                copy.wait_send()
+
+
+class Exchange:
+    def __init__(self, net, sent, got, peer):
+        self.net, self.sent, self.got, self.peer = net, sent, got, peer
+        self.base = net.reserve(ROWS // STEP_ROWS, self)
+
+    def copy(self, k):
+        r = pl.ds(pl.multiple_of(k * STEP_ROWS, STEP_ROWS), STEP_ROWS)
+        return pltpu.make_async_remote_copy(
+            src_ref=self.sent.at[r, :], dst_ref=self.got.at[r, :],
+            send_sem=self.net.send.at[self.base + k], recv_sem=self.net.recv.at[self.base + k],
+            device_id=self.peer, device_id_type=MESH_IDS,
+        )
+
+    def give(self, fn):
+        def body(k, carry):
+            r = pl.ds(pl.multiple_of(k * STEP_ROWS, STEP_ROWS), STEP_ROWS)
+            self.sent[r, :] = fn(r).astype(LOW)
+            self.copy(k).start()
+            return carry
+
+        lax.fori_loop(0, ROWS // STEP_ROWS, body, 0)
+
+    def take(self, fn):
+        def body(k, carry):
+            r = pl.ds(pl.multiple_of(k * STEP_ROWS, STEP_ROWS), STEP_ROWS)
+            self.copy(k).wait_recv()
+            fn(r, self.sent[r, :].astype(F32) + self.got[r, :].astype(F32))
+            return carry
+
+        lax.fori_loop(0, ROWS // STEP_ROWS, body, 0)
+
+    def wait_send(self):
+        for k in range(ROWS // STEP_ROWS):
+            self.copy(k).wait_send()
 
 
 def padded_width(w):
@@ -819,12 +871,12 @@
 
 
 def forward_body(
-    w_in, w_back, w_up, w_down, seg_col, seg_row, norms, side, embed, level, tokens, noises, codecs,
+    w_in, w_back, w_up, w_down, segments, norms, steps, tokens, noises, codecs,
     g0, g1, g2, g3, g4, sq, n1_o, qkv_o, mixed_o, logs_o, resid_o, n2_o, noisy_o, first_o, conv_o,
     taps_o, resid3_o, n3_o, cq_o, ckv_o, cross_o, logs_c_o, out_o,
     p0, p1, p2, p3, p4, v0, v1, v2, v3, v4, tok, noise, codec, n1, qkv, mixed, logs, resid, n2,
     noisy, conv, taps, resid3, n3, cq, ckv, cross, logs_c, out, pad, acc, sent, got,
-    part, near, far_out, far_in, summed,
+    part, near, far_out, far_in, summed, seg_col,
     in_sem, out_sem, own_sem, send, recv,
 ):
     pieces, held, kept = (p0, p1, p2, p3, p4), (v0, v1, v2, v3, v4), (g0, g1, g2, g3, g4)
@@ -835,7 +887,7 @@
     heads = n // HD
     score_scale = HD ** (-0.5)
     net = Sender(send, recv)
-    run = Gather(pieces, held, (2, 4, 0, 0, 2), (3,), net)
+    run = Gather(pieces, held, (2, 4, 0, 0, 0), (3,), net)
     share = Share(net, pad, TIME)
     total_sum = FourSum(net, part, near, far_out, far_in, summed)
     x, core, z, y = place()
@@ -860,13 +912,8 @@
         copy.start()
         return copy
 
-    def exchange(k, total):
-        sent[k] = total.astype(LOW)
-        return net.start(sent.at[k], got.at[k], sibling)
-
-    def joined(k, r):
-        return sent[k, r, :].astype(F32) + got[k, r, :].astype(F32)
-
+    side = own_channels(norms, 2 * x + core, n)
+    level = steps[2:3, 0:1]
     local = [pack(0)]
     meet([run.to_x, run.to_y, *z_peers(), sibling])
     run.line(0)
@@ -908,8 +955,10 @@
     store(qkv, qkv_o)
     run.spread(1, 3)
 
+    seg_row = own_segments(segments, x, seg_col)
+
     def self_heads(r):
-        mask = seg_col[r, :] == seg_row[...]
+        mask = seg_col[r, :] == seg_row
         found = []
         for i in range(2):
             part, logs_i = softmax_heads(
@@ -918,12 +967,12 @@
             mixed[i, r, :] = part
             found += logs_i
         logs[r, :] = jnp.concatenate(found, axis=1)
-
-    each_rows(self_heads)
-    swap = exchange(
-        0,
-        mm_nt(mixed[0], matrix_of(v0, 0, 3 * n, 4 * n)) + mm_nt(mixed[1], matrix_of(v0, 1, 3 * n, 4 * n)),
-    )
+        return mm_nt(mixed[0, r, :], matrix_of(v0, 0, 3 * n, 4 * n)) + mm_nt(
+            mixed[1, r, :], matrix_of(v0, 1, 3 * n, 4 * n)
+        )
+
+    swap = Exchange(net, sent.at[0], got.at[0], sibling)
+    swap.give(self_heads)
     store(mixed, mixed_o)
     store(logs, logs_o)
     run.relay(2)
@@ -932,15 +981,14 @@
     run.turn(1)
     run.own(4)
     run.line(4)
-    swap.wait_recv()
-
-    def norm_two(r):
-        v = tok[r, :].astype(F32) + joined(0, r)
+
+    def norm_two(r, both):
+        v = tok[r, :].astype(F32) + both
         resid[r, :] = v
         hat, _ = ln_stats(v)
         n2[r, :] = (hat * norms[2:3, :] + norms[3:4, :]).astype(LOW)
 
-    each_rows(norm_two)
+    swap.take(norm_two)
     store(resid, resid_o)
     store(n2, n2_o)
     run.spread(2, 3)
@@ -958,14 +1006,14 @@
                 acc[...] = term
             else:
                 acc[...] += term
-    swap = exchange(1, acc[...])
+    swap = Exchange(net, sent.at[1], got.at[1], sibling)
+    swap.give(lambda r: acc[r, :])
     loads[1].wait()
-    swap.wait_recv()
-
-    def add_noise(r):
-        noisy[r, :] = resid[r, :] + joined(1, r) + level[...] * noise[r, :].astype(F32)
-
-    each_rows(add_noise)
+
+    def add_noise(r, both):
+        noisy[r, :] = resid[r, :] + both + level * noise[r, :].astype(F32)
+
+    swap.take(add_noise)
     store(noisy, noisy_o)
     mats = group_mats(features, width)
     mats_n = group_mats(n, width)
@@ -987,8 +1035,6 @@
     lax.fori_loop(0, ROWS // STEP_ROWS, act, 0)
     share.begin()
     run.relay(4)
-    run.spread(4, 1)
-    run.spread(4, 2)
     local[2].wait()
     run.ready(2)
     store(v2, g2)
@@ -1000,7 +1046,8 @@
                 pad[i, TIME * a : TIME * a + ROWS, :], matrix_of(v2, 0, 3 * n * a, 3 * n * (a + 1))
             )
             q = term if q is None else q + term
-        shift = mm(embed[i], matrix_of(v2, 0, 9 * n, 10 * n))[0:1]
+        embed = jnp.broadcast_to(steps[i : i + 1, :], (8, features)).astype(LOW)
+        shift = mm(embed, matrix_of(v2, 0, 9 * n, 10 * n))[0:1]
         c1 = from_left(q[:, :n]) + q[:, n : 2 * n] + from_right(q[:, 2 * n :]) + shift
         conv[i] = c1
         c1 = c1 - group_average(jnp.sum(c1, axis=0, keepdims=True), mats_n, width)
@@ -1025,6 +1072,8 @@
 
     conv_layer(0)
     share.pass_on()
+    run.spread(4, 1)
+    run.spread(4, 2)
     run.spread(4, 3)
     share.end()
     store(pad.at[:, pl.ds(TIME, ROWS), :], first_o)
@@ -1068,27 +1117,26 @@
             cross[i, r, :] = part
             found += logs_i
         logs_c[r, :] = jnp.concatenate(found, axis=1)
-
-    each_rows(cross_heads)
-    swap = exchange(
-        2,
-        mm_nt(cross[0], matrix_of(v4, 0, 3 * n, 4 * n)) + mm_nt(cross[1], matrix_of(v4, 1, 3 * n, 4 * n)),
-    )
+        return mm_nt(cross[0, r, :], matrix_of(v4, 0, 3 * n, 4 * n)) + mm_nt(
+            cross[1, r, :], matrix_of(v4, 1, 3 * n, 4 * n)
+        )
+
+    swap = Exchange(net, sent.at[2], got.at[2], sibling)
+    swap.give(cross_heads)
     store(cross, cross_o)
     store(logs_c, logs_c_o)
-    swap.wait_recv()
-
-    def finish_rows(r):
-        out[r, :] = (resid3[r, :] + joined(2, r)).astype(LOW)
-
-    each_rows(finish_rows)
+
+    def finish_rows(r, both):
+        out[r, :] = (resid3[r, :] + both).astype(LOW)
+
+    swap.take(finish_rows)
     store(out, out_o)
     for c in stores:
         c.wait()
     net.close()
 
 
-def forward_all(w_in, w_back, w_up, w_down, seg_col, seg_row, norms, side, embed, level, tokens, noises, codecs):
+def forward_all(w_in, w_back, w_up, w_down, segments, norms, steps, tokens, noises, codecs):
     n, hid = w_in.shape[2], w_up.shape[1]
     rows, features = w_in.shape[1], norms.shape[1]
     heads = 2 * n // HD
@@ -1104,11 +1152,11 @@
     ]
     groups = [(2 - (g in (2, 3)), 4, 2, rows, w) for g, w in enumerate(widths)]
     dma = pltpu.SemaphoreType.DMA
-    copies = 3 * 13 + 7 + 4 + 3 + 2 + 4
+    copies = 3 * 13 + 7 + 4 + 12 + 2 + 4
     res = pl.pallas_call(
         forward_body,
         name="forward",
-        in_specs=[spec_vm() for _ in range(10)] + [spec_any() for _ in range(3)],
+        in_specs=[spec_vm() for _ in range(7)] + [spec_any() for _ in range(3)],
         out_specs=[spec_any() for _ in groups] + [spec_vm()] + [spec_any() for _ in kept],
         out_shape=[jax.ShapeDtypeStruct(s, LOW) for s in groups]
         + [jax.ShapeDtypeStruct((1, 128), F32)]
@@ -1118,13 +1166,13 @@
             VM(full, LOW), VM(full, LOW), VM((ctok, features), LOW), *[VM(s, t) for k, (s, t) in enumerate(kept) if k != 7],
             VM((2, tall, features), LOW), VM(full, F32), VM((3, *full), LOW), VM((3, *full), LOW),
             VM((2, *full), LOW), VM((2, ROWS // 2, features), LOW), VM((ROWS // 2, features), LOW),
-            VM((ROWS // 2, features), LOW), VM(full, LOW),
+            VM((ROWS // 2, features), LOW), VM(full, LOW), VM((ROWS, 1), F32),
             dma((3,)), dma((22,)), dma((5,)), dma((copies,)), dma((copies,)),
         ],
         compiler_params=pltpu.CompilerParams(
             collective_id=0, has_side_effects=True, vmem_limit_bytes=62 << 20
         ),
-    )(w_in, w_back, w_up, w_down, seg_col, seg_row, norms, side, embed, level, tokens, noises, codecs)
+    )(w_in, w_back, w_up, w_down, segments, norms, steps, tokens, noises, codecs)
     return res[:5], res[5], res[6:]
 
 
@@ -1260,14 +1308,14 @@
 
 
 def backward_body(
-    seg_col, seg_row, norms, side, embed_rows, sq, tokens, cots, codecs,
+    segments, norms, steps, sq, tokens, cots, codecs,
     g0, g1, g2, g3, g4, n1_h, qkv_h, mixed_h, logs_h, resid_h, n2_h, noisy_h, first_h, conv_h, taps_h,
     resid3_h, n3_h, cq_h, ckv_h, cross_h, logs_c_h, out_h,
-    s0, s1, s2, s3, s4, grad_x, other_x, other_out, rows_o,
+    s0, s1, s2, s3, s4, all_x, all_out, rows_o,
     d_c, d_t, d_o, d_m, wv, cot, codec, cq, ckv, cross, gm, logs, resid, nrm, grad, pad, taps, tapsg,
     conv, first, hb, hb2, acc, sent, got, part, near, far_out, far_in, summed,
     f1_c, f2_c, fy_c, pair_c, fx_c, ly_t, r1_t, r2_t, f1_o, f2_o, fy_o,
-    ly_m, r1_m, r2_m, lx_m, co_m, ly_a, r1_a, r2_a, lx_a, co_a, values, values_in,
+    ly_m, r1_m, r2_m, lx_m, co_m, ly_a, r1_a, r2_a, lx_a, co_a, values, values_in, seg_col,
     stage, gsum, load_sem, out_sem, send, recv,
 ):
     n = cq.shape[2]
@@ -1296,6 +1344,9 @@
 
     own = pl.ds(pl.multiple_of(x * ROWS, ROWS), ROWS)
     half = pl.ds(pl.multiple_of(core * (ROWS // 2), ROWS // 2), ROWS // 2)
+    mine = pl.ds(pl.multiple_of(x * ROWS + core * (ROWS // 2), ROWS // 2), ROWS // 2)
+    brought = pl.ds(pl.multiple_of((1 - x) * ROWS + core * (ROWS // 2), ROWS // 2), ROWS // 2)
+    side = own_channels(norms, 2 * x + core, n)
     ready = [
         load(cots.at[own, :], cot), load(cross_h, cross), load(g4.at[0], wv.at[0, :, pl.ds(0, 4 * n)]),
         load(g4.at[1], wv.at[1, :, pl.ds(0, 4 * n)]), load(cq_h, cq), load(ckv_h, ckv),
@@ -1303,7 +1354,9 @@
     ]
     later = [load(resid3_h, resid), load(taps_h, taps), load(conv_h, conv), load(first_h, first)]
     meet([to_x, to_y, *z_peers(), sibling])
-    out_far = net.start(out_h.at[half, :], other_out.at[half, :], to_x)
+    out_far = net.start(out_h.at[half, :], all_out.at[mine, :], to_x)
+    out_own = pltpu.make_async_copy(out_h, all_out.at[own, :], out_sem.at[8])
+    out_own.start()
     sends = {}
     cro = ScatterZ(net, d_c, (f1_c, f2_c, fy_c, pair_c, fx_c))
     two = Scatter(net, d_t, 0, (ly_t, r1_t, r2_t))
@@ -1318,14 +1371,11 @@
     share = Share(net, pad, TIME)
     total_sum = FourSum(net, part, near, far_out, far_in, summed)
 
-    def exchange(k, total):
+    def exchange(k):
         if k >= 2:
             sends[k - 2].wait_send()
-        sent[k % 2] = total.astype(LOW)
-        sends[k] = net.start(sent.at[k % 2], got.at[k % 2], sibling)
-
-    def joined(k, r):
-        return sent[k % 2, r, :].astype(F32) + got[k % 2, r, :].astype(F32)
+        sends[k] = Exchange(net, sent.at[k % 2], got.at[k % 2], sibling)
+        return sends[k]
 
     def put(ref, i, first, value):
         w = value.shape[1]
@@ -1349,9 +1399,9 @@
             )
             cq[i, r, :] = gq.astype(LOW)
             acc_kv[:, 2 * n * i : 2 * n * (i + 1)] += jnp.concatenate([gk, gv], axis=1)
-
-    each_rows(cross_heads)
-    exchange(0, mm_nt(cq[1], wv[1, :, :n]) + mm_nt(cq[0], wv[0, :, :n]))
+        return mm_nt(cq[1, r, :], wv[1, :, :n]) + mm_nt(cq[0, r, :], wv[0, :, :n])
+
+    exchange(0).give(cross_heads)
     for i in (1, 0):
         both = acc_kv[:, 2 * n * i : 2 * n * (i + 1)]
         low = jnp.concatenate([both[:, :n] * score_scale, both[:, n:]], axis=1).astype(LOW)
@@ -1368,17 +1418,16 @@
     other_grad = pad.at[1, TIME : TIME + ROWS, :]
     for c in later:
         c.wait()
-    sends[0].wait_recv()
-
-    def pull_three(r):
-        back, gain, shift = ln_back(resid[r, :], norms[8:9, :], joined(0, r))
+
+    def pull_three(r, both):
+        back, gain, shift = ln_back(resid[r, :], norms[8:9, :], both)
         v = cot[r, :].astype(F32) + back
         grad[r, :] = v
         low_grad[r, :] = v.astype(LOW)
         rows[8:9, :] += gain
         rows[9:10, :] += shift
 
-    each_rows(pull_three)
+    sends[0].take(pull_three)
     share.begin()
     tok_load = load(tokens.at[own, :], cot)
     noisy_load = load(noisy_h, resid)
@@ -1432,7 +1481,7 @@
 
     conv_pull(0)
     out_far.wait_recv()
-    out_near = net.start(other_out.at[half, :], other_out.at[half, :], sibling)
+    out_near = net.start(all_out.at[brought, :], all_out.at[brought, :], sibling)
     share.pass_on()
     share.end()
     conv_pull(1)
@@ -1462,7 +1511,7 @@
     put(
         d_o, 0, 9 * n,
         lax.dot_general(
-            embed_rows[...], gsum[...], (((0,), (0,)), ((), ())), precision=HIGHEST_PRECISION,
+            steps[...], gsum[...], (((0,), (0,)), ((), ())), precision=HIGHEST_PRECISION,
             preferred_element_type=F32,
         ),
     )
@@ -1518,7 +1567,7 @@
             else:
                 acc[...] += term
         if q == len(mlp) - 1:
-            exchange(1, acc[...])
+            exchange(1).give(lambda r: acc[r, :])
         for i in (1, 0):
             put(d_m.at[q], i, block, mm_tn(low_grad[...], hb[i]))
             put(d_m.at[q], i, 0, mm_tn(nrm[...], hb2[i]))
@@ -1530,25 +1579,26 @@
         load(n1_h, nrm), load(qkv_h, tapsg.at[:, pl.ds(0, ROWS), :]), load(mixed_h, cross), load(logs_h, logs),
     ]
     resid_load.wait()
-    sends[1].wait_recv()
-
-    def pull_one(r):
-        back, g_gain, g_shift = ln_back(resid[r, :], norms[2:3, :], joined(1, r))
+
+    def pull_one(r, both):
+        back, g_gain, g_shift = ln_back(resid[r, :], norms[2:3, :], both)
         v = grad[r, :] + back
         grad[r, :] = v
         low_grad[r, :] = v.astype(LOW)
         rows[2:3, :] += g_gain
         rows[3:4, :] += g_shift
 
-    each_rows(pull_one)
+    sends[1].take(pull_one)
     for c in (*attn_w, *tail_loads):
         c.wait()
     for i in range(2):
         gm[i] = mm(low_grad[...], wv[i, :, 3 * n : 4 * n]).astype(LOW)
     acc[...] = jnp.zeros(acc.shape, F32)
 
+    seg_row = own_segments(segments, x, seg_col)
+
     def self_heads(r):
-        mask = seg_col[r, :] == seg_row[...]
+        mask = seg_col[r, :] == seg_row
         for i in range(2):
             rows_logs = [logs[r, heads * i + h : heads * i + h + 1] for h in range(heads)]
             gq, gk, gv = softmax_heads_back(
@@ -1568,24 +1618,23 @@
         put(d_c, i, 3 * n, mm_tn(low_grad[...], cross[i]))
         put(d_c, i, 0, mm_tn(nrm[...], taps[i, 0:ROWS, :]))
     attn.raw()
-    exchange(
-        2, mm_nt(taps[1, 0:ROWS, :], wv[1, :, : 3 * n]) + mm_nt(taps[0, 0:ROWS, :], wv[0, :, : 3 * n])
+    exchange(2).give(
+        lambda r: mm_nt(taps[1, r, :], wv[1, :, : 3 * n]) + mm_nt(taps[0, r, :], wv[0, :, : 3 * n])
     )
     two.lines()
     tok_load.wait()
-    sends[2].wait_recv()
-
-    def pull_zero(r):
-        back, g_gain, g_shift = ln_back(cot[r, :].astype(F32), norms[0:1, :], joined(2, r))
+
+    def pull_zero(r, both):
+        back, g_gain, g_shift = ln_back(cot[r, :].astype(F32), norms[0:1, :], both)
         low_grad[r, :] = (grad[r, :] + back).astype(LOW)
         rows[0:1, :] += g_gain
         rows[1:2, :] += g_shift
 
-    each_rows(pull_zero)
-    store_x = pltpu.make_async_copy(low_grad, grad_x, out_sem.at[5])
+    sends[2].take(pull_zero)
+    store_x = pltpu.make_async_copy(low_grad, all_x.at[own, :], out_sem.at[5])
     store_x.start()
     middle = pl.ds(pl.multiple_of(TIME + core * (ROWS // 2), TIME), ROWS // 2)
-    x_far = net.start(pad.at[0, middle, :], other_x.at[half, :], to_x)
+    x_far = net.start(pad.at[0, middle, :], all_x.at[mine, :], to_x)
     rows[0:6, :] = jnp.where(core == 0, rows[0:6, :], 0.0)
     rows[8:10, :] = jnp.where(core == 0, rows[8:10, :], 0.0)
     totals.start(0)
@@ -1614,7 +1663,7 @@
     attn.corners()
     totals.step(3)
     x_far.wait_recv()
-    x_near = net.start(other_x.at[half, :], other_x.at[half, :], sibling)
+    x_near = net.start(all_x.at[brought, :], all_x.at[brought, :], sibling)
     mlp[1].half()
     deliver(one, 2, s2)
     attn.lines()
@@ -1629,18 +1678,19 @@
     out_near.wait_recv()
     x_near.wait_recv()
     store_x.wait()
+    out_own.wait()
     wait_sends(net, [sends[0], share.far, *cro.sent])
 
 
 def wait_sends(net, done):
     for copy in net.made:
-        if all(copy is not d for d in done):
+        if copy is not None and all(copy is not d for d in done):
             copy.wait_send()
 
 
-def backward_all(seg_col, seg_row, norms, side, embed_rows, sq, tokens, cots, codecs, gathered, kept):
+def backward_all(segments, norms, steps, sq, tokens, cots, codecs, gathered, kept):
     features = norms.shape[1]
-    n = side.shape[1]
+    n = kept[2].shape[2]
     rows = gathered[0].shape[3]
     widths = [g.shape[4] for g in gathered]
     hid = widths[1] // 2
@@ -1649,7 +1699,7 @@
     full = (ROWS, features)
     tall = ROWS + 2 * TIME
     ins = [
-        seg_col, seg_row, norms, side, embed_rows, sq, tokens, cots, codecs,
+        segments, norms, steps, sq, tokens, cots, codecs,
         *[g.reshape(g.shape[0], features, -1) for g in gathered], *kept,
     ]
     dma = pltpu.SemaphoreType.DMA
@@ -1660,17 +1710,17 @@
     def pieces(width, *counts):
         return [VM((*(k if isinstance(k, tuple) else (k,)), rows, width), LOW) for k in counts]
 
-    copies = 2 + 3 + 2 + 2 + 4 + 5 + 5 + 4 + 4 + parts * 9 + 9
+    copies = 2 + 12 + 2 + 2 + 4 + 5 + 5 + 4 + 4 + parts * 9 + 9
     res = pl.pallas_call(
         backward_body,
         name="backward",
-        in_specs=[spec_vm() for _ in range(6)] + [spec_any() for _ in ins[6:]],
-        out_specs=[spec_any() for _ in range(8)] + [spec_vm()],
+        in_specs=[spec_vm() for _ in range(4)] + [spec_any() for _ in ins[4:]],
+        out_specs=[spec_any() for _ in range(7)] + [spec_vm()],
         out_shape=[
             jax.ShapeDtypeStruct((parts, rows, 2 * block) if g == 1 else (rows, w), F32)
             for g, w in enumerate(widths)
         ]
-        + [jax.ShapeDtypeStruct(full, LOW)] * 3
+        + [jax.ShapeDtypeStruct((2 * ROWS, features), LOW)] * 2
         + [jax.ShapeDtypeStruct((16, features), F32)],
         scratch_shapes=[
             VM((2, 4, 2, rows, 4 * n), LOW), VM((1, 4, 2, rows, widths[3]), LOW),
@@ -1688,15 +1738,15 @@
             *pieces(10 * n, (2, 1, 2), (1, 2), 1),
             *pieces(2 * block, (parts, 4), (parts, 2), parts, (parts, 4), (parts, 4)),
             *pieces(4 * n, 4, 2), VM((rows, 4 * n), LOW), *pieces(4 * n, 4, 4),
-            VM((6, 16, features), F32), VM((5, 16, features), F32),
+            VM((6, 16, features), F32), VM((5, 16, features), F32), VM((ROWS, 1), F32),
             VM((rows, 10 * n), F32), VM((8, n), F32),
-            dma((30,)), dma((8,)), dma((copies,)), dma((copies,)),
+            dma((30,)), dma((9,)), dma((copies,)), dma((copies,)),
         ],
         compiler_params=pltpu.CompilerParams(
             collective_id=1, has_side_effects=True, vmem_limit_bytes=64 << 20
         ),
     )(*ins)
-    return res[:5], res[5], res[6], res[7], res[8]
+    return res[:5], res[5], res[6], res[7]
 
 
 def adam_rows(w, g, m, v, decay_rate):
@@ -1707,44 +1757,77 @@
     return m_new, v_new, update
 
 
+def moment_chunks(masters):
+    chunks = []
+    for a, size in ((0, 4), (1, 4)):
+        count = masters[a].shape[0]
+        chunks += [(a, k, min(k + size, count)) for k in range(0, count, size)]
+    return chunks + [(2, 0, 1), (3, 0, 1)]
+
+
 def moments_body(*refs):
+    sums_h, refs = refs[:5], refs[5:]
+    w_h, m_h, v_h, refs = refs[:4], refs[4:8], refs[8:12], refs[12:]
+    nm_h, nv_h, u_h, usq, refs = refs[:4], refs[4:8], refs[8:12], refs[12], refs[13:]
     sums, refs = refs[:5], refs[5:]
-    w_in, w_back, w_up, w_down, m_in, m_back, m_up, m_down, v_in, v_back, v_up, v_down = refs[:12]
-    nm_in, nm_back, nm_up, nm_down, nv_in, nv_back, nv_up, nv_down = refs[12:20]
-    u_in, u_back, u_up, u_down, usq = refs[20:]
-    n = w_in.shape[2]
+    w, m, v, nm, nv, u, (in_sem, out_sem) = (
+        refs[:4], refs[4:8], refs[8:12], refs[12:16], refs[16:20], refs[20:24], refs[24:]
+    )
+    n = w[0].shape[2]
+    chunks = moment_chunks(w)
+    copies = []
+
+    def part(ref, chunk):
+        return ref.at[chunk[1] : chunk[2]] if chunk[0] < 2 else ref
+
+    def load(src, dst):
+        copy = pltpu.make_async_copy(src, dst, in_sem.at[len(copies)])
+        copy.start()
+        copies.append(copy)
+        return copy
+
+    sum_loads = [load(sums_h[g], sums[g]) for g in range(5)]
+    loads = [
+        [load(part(h[c[0]], c), part(r[c[0]], c)) for h, r in ((w_h, w), (m_h, m), (v_h, v))]
+        for c in chunks
+    ]
+    where_in, where_back = {}, {}
+    for g, (ins, backs) in GROUPS_OF.items():
+        where_in.update({j: (g, k) for k, j in enumerate(ins)})
+        where_back.update({j: (g, k) for k, j in enumerate(backs, len(ins))})
     squares = [None] * 29
-
-    def place_in(j, g):
-        m, v, u = adam_rows(w_in[j], g, m_in[j], v_in[j], WEIGHT_DECAY)
-        nm_in[j], nv_in[j], u_in[j] = m, v, u
-        squares[j] = square_sum(u)
-
-    def place_back(j, g):
-        m, v, u = adam_rows(w_back[j], g.T, m_back[j], v_back[j], WEIGHT_DECAY)
-        nm_back[j], nv_back[j], u_back[j] = m, v, u
-        squares[16 + j] = square_sum(u)
-
-    for g, (ins, backs) in GROUPS_OF.items():
-        for k, j in enumerate(ins):
-            place_in(j, sums[g][:, n * k : n * (k + 1)])
-        for k, j in enumerate(backs, len(ins)):
-            place_back(j, sums[g][:, n * k : n * (k + 1)])
-    block = sums[1].shape[2] // 2
-    up_sq, down_sq = [], []
-    for q in range(w_up.shape[1] // block):
-        cols = slice(block * q, block * (q + 1))
-        m, v, u = adam_rows(w_up[:, cols], sums[1][q, :, :block], m_up[:, cols], v_up[:, cols], WEIGHT_DECAY)
-        nm_up[:, cols], nv_up[:, cols], u_up[:, cols] = m, v, u
-        up_sq.append(square_sum(u))
-        m, v, u = adam_rows(
-            w_down[:, cols], sums[1][q, :, block:], m_down[:, cols], v_down[:, cols], WEIGHT_DECAY
-        )
-        nm_down[:, cols], nv_down[:, cols], u_down[:, cols] = m, v, u
-        down_sq.append(square_sum(u))
-    squares[27] = sum(up_sq)
-    squares[28] = sum(down_sq)
+    for s in sum_loads:
+        s.wait()
+    stores = []
+    for c, waits in zip(chunks, loads):
+        for s in waits:
+            s.wait()
+        a = c[0]
+        if a < 2:
+            for j in range(c[1], c[2]):
+                g, k = (where_back if a else where_in)[j]
+                grad = sums[g][:, n * k : n * (k + 1)]
+                grad = grad.T if a else grad
+                nm[a][j], nv[a][j], u[a][j] = adam_rows(w[a][j], grad, m[a][j], v[a][j], WEIGHT_DECAY)
+                squares[16 * a + j] = square_sum(u[a][j])
+        else:
+            block = sums[1].shape[2] // 2
+            found = []
+            for q in range(w[a].shape[1] // block):
+                cols = slice(block * q, block * (q + 1))
+                grad = sums[1][q, :, block * (a - 2) : block * (a - 1)]
+                nm[a][:, cols], nv[a][:, cols], u[a][:, cols] = adam_rows(
+                    w[a][:, cols], grad, m[a][:, cols], v[a][:, cols], WEIGHT_DECAY
+                )
+                found.append(square_sum(u[a][:, cols]))
+            squares[25 + a] = sum(found)
+        for r, h in ((nm, nm_h), (nv, nv_h), (u, u_h)):
+            copy = pltpu.make_async_copy(part(r[a], c), part(h[a], c), out_sem.at[len(stores)])
+            copy.start()
+            stores.append(copy)
     usq[...] = row_of(squares)
+    for copy in stores:
+        copy.wait()
 
 
 def totals_body(usq, out, ring, ring_b, send, recv):
@@ -1796,10 +1879,23 @@
 
 def lamb_all(sums, rows, masters, moments, squares, norms, norm_m, norm_v):
     shapes = [(v.shape, F32) for v in masters]
-    *mvu, usq = run_kernel(
-        moments_body, "lamb_moments", [*sums, *masters, *moments, *squares],
-        [*shapes, *shapes, *shapes, ((1, 128), F32)], [],
-    )
+    dma = pltpu.SemaphoreType.DMA
+    ins = [*sums, *masters, *moments, *squares]
+    runs = len(moment_chunks(masters))
+    *mvu, usq = pl.pallas_call(
+        moments_body,
+        name="lamb_moments",
+        in_specs=[spec_any() for _ in ins],
+        out_specs=[spec_any() for _ in range(12)] + [spec_vm()],
+        out_shape=[jax.ShapeDtypeStruct(v.shape, F32) for v in masters * 3]
+        + [jax.ShapeDtypeStruct((1, 128), F32)],
+        scratch_shapes=[
+            *[VM(v.shape, F32) for v in sums], *[VM(v.shape, F32) for v in masters * 6],
+            dma((5 + 3 * runs,)), dma((3 * runs,)),
+        ],
+        compiler_params=pltpu.CompilerParams(vmem_limit_bytes=50 << 20),
+        cost_estimate=pl.CostEstimate(flops=2 * 10**7, bytes_accessed=21 * 10**6, transcendentals=10**6),
+    )(*ins)
     dma = pltpu.SemaphoreType.DMA
     usq_sum = pl.pallas_call(
         totals_body,
@@ -1841,30 +1937,22 @@
     norm_v,
 ):
     features = tokens.shape[1]
-    n = w_in.shape[2]
     mp = lax.axis_index("mp")
-    dp = lax.axis_index("dp")
-    x, core, z, y = mp // 2, mp % 2, dp // 2, dp % 2
-
-    steps = by_parity(x, timesteps[0], timesteps[1], 0)
-    seg = pick(segments, x, 0)
-    seg_col, seg_row = seg[:, None], seg[None, :]
-    noise_level = jnp.sqrt((steps[0].astype(F32) + 1.0) / TSTEPS).reshape(1, 1)
-    embed = jax.nn.silu(time_embedding(steps, features)).astype(LOW)
-    embed_rows = jnp.broadcast_to(embed[:, None], (2, 8, features))
-    embed_eight = jnp.pad(embed.astype(F32), ((0, 6), (0, 0)))
-    side = lax.dynamic_slice(norm_params, (6, (2 * x + core) * n), (2, n))
-    norms = norm_params
-
+    x = mp // 2
+
+    both = jnp.where(x == 0, timesteps, timesteps[::-1])
+    embed = jax.nn.silu(time_embedding(both, features)).astype(LOW).astype(F32)
+    level = jnp.sqrt((both[:1].astype(F32) + 1.0) / TSTEPS)
+    row = lax.broadcasted_iota(jnp.int32, (8, features), 0)
+    steps = jnp.where(row == 0, embed[0:1], jnp.where(row == 1, embed[1:2], level))
     gathered, weight_sq, kept = forward_all(
-        w_in, w_back, w_up, w_down.T, seg_col, seg_row, norms, side, embed_rows, noise_level,
-        tokens, noise_field, codec_tokens,
-    )
-    sums, own_x, other_x, other_out, rows = backward_all(
-        seg_col, seg_row, norms, side, embed_eight, weight_sq, tokens, cotangent, codec_tokens, gathered, kept
-    )
-    out_rows = by_parity(x, kept[-1], other_out, 0).reshape(-1, features)
-    grad_rows = by_parity(x, own_x, other_x, 0).reshape(-1, features).astype(F32)
+        w_in, w_back, w_up, w_down.T, segments, norm_params, steps, tokens, noise_field, codec_tokens
+    )
+    gsteps = jnp.where(row < 2, steps, 0.0)
+    sums, all_x, out_rows, rows = backward_all(
+        segments, norm_params, gsteps, weight_sq, tokens, cotangent, codec_tokens, gathered, kept
+    )
+    grad_rows = all_x.astype(F32)
     stepped = lamb_all(
         sums, rows, (w_in, w_back, w_up, w_down.T), (m_in, m_back, m_up, m_down.T),
         (v_in, v_back, v_up, v_down.T), norm_params, norm_m, norm_v,

time: 418 us -> 406 us (0.971)
  Pallas kernels: 395 us -> 389 us
    pallas_call x2 -> x1, Pallas kernels: 16.5 us -> 4.93 us  [run_kernel(): pl.pallas_call(body, name=name, in_specs=in_specs, out_specs=[spec_vm() f...]
    pallas_call x0 -> x1, Pallas kernels: none -> 7.91 us  [lamb_all(): pl.pallas_call(moments_body, name='lamb_moments', in_specs=[spec_any() fo...]
where the time goes in v1:
time: 406 us; the launch traced here: 400 us
  Pallas kernels  389 us (96%)
  other arithmetic  4.97 us (1%)
    pallas_call x1, Pallas kernels, backward_all(): pl.pallas_call(backward_body, name='backward', in_specs=[spec_vm() for _...  194 us
    pallas_call x1, Pallas kernels, forward_all(): pl.pallas_call(forward_body, name='forward', in_specs=[spec_vm() for _ in...  173 us
    pallas_call x1, Pallas kernels, lamb_all(): pl.pallas_call(totals_body, name='norm_totals', in_specs=[spec_vm()], out...  10.3 us

profile of v1, /device:TPU:0, one launch (start us, length us, event | category | flops | bytes accessed | tf_op | source)
XLA Modules:
  0.0 399.5 jit_solution(17560770189967558110)
XLA Ops:
  0.7 0.7 rev.3
  1.4 0.7 fusion.2
  2.2 0.1 multiply_sine_fusion
  2.4 0.7 select_select_fusion
  3.1 172.6 %forward.1 = (bf16[2,4,2,96,768]{4,3,2,1,0:T(8,128)(2,1)}, bf16[2,4,2,96,1536]{4,3,2,1,0:T(8,128)(2,1)}, bf16[1,4,2,96,1920]{4,3,2,1,0:T(8,128)(2,1)}, bf16[1,4,...) custom-call(f32[16,96,192]{2,1,0:T(8,128)} %w_in.3, ...), custom_call_target="tpu_custom_call" | custom-call | tf_op jit(solution)/shard_map/forward/pallas_call | solution.py:1156
  175.7 193.6 %backward.1 = (f32[96,768]{1,0:T(8,128)}, f32[3,96,512]{2,1,0:T(8,128)}, f32[96,1920]{1,0:T(8,128)}, f32[96,1792]{1,0:T(8,128)}, f32[96,768]{1,0:T(8,128)}, /*in...) custom-call(s32[2,512]{1,0:T(2,128)} %segments.3, f32[10,768]{1,0:T(8,128)} %norms.5, ...), custom_call_target="tpu_custom_call" | custom-call | tf_op jit(solution)/shard_map/backward/pallas_call | solution.py:1714
  369.2 0.0 copy-start
  369.2 0.0 copy-start.1
  369.3 0.0 copy-start.2
  369.3 0.0 copy-start.3
  369.3 0.0 copy-start.4
  369.3 0.0 copy-start.5
  369.3 0.0 copy-start.6
  369.3 0.0 copy-start.7
  369.3 0.0 copy-start.8
  369.3 3.5 convert_element_type.19
  372.8 0.0 copy-done
  372.8 0.0 copy-done.1
  372.8 0.0 copy-done.2
  372.8 0.0 copy-done.3
  372.8 0.0 copy-done.4
  372.8 0.0 copy-done.5
  372.8 0.0 copy-done.6
  372.8 0.0 copy-done.7
  372.9 0.0 copy-done.8
  372.9 7.9 %lamb_moments.1 = (f32[16,96,192]{2,1,0:T(8,128)}, f32[11,192,96]{2,1,0:T(8,128)}, f32[96,768]{1,0:T(8,128)}, f32[96,768]{1,0:T(8,128)}, f32[16,96,192]{2,1,0:T(...) custom-call(f32[96,768]{1,0:T(8,128)S(1)} %copy-done.7, ...), custom_call_target="tpu_custom_call" | custom-call | flops 20000000 | bytes 21000000 | tf_op jit(solution)/shard_map/lamb_moments/pallas_call | solution.py:1885
  380.8 0.0 copy-start.9
  380.8 0.7 copy-done.9
  381.5 0.0 copy-start.10
  381.5 0.7 copy-done.10
  382.2 0.0 copy-start.11
  382.2 0.5 copy-done.11
  382.7 10.3 %norm_totals.1.sums = f32[8,128]{1,0:T(8,128)} custom-call(f32[1,128]{1,0:T(1,128)} %copy-done.11), custom_call_target="tpu_custom_call" | custom-call | tf_op jit(solution)/shard_map/norm_totals/pallas_call | solution.py:1900
  393.0 0.0 copy-start.12
  393.0 4.9 %lamb_apply.1 = (f32[16,96,192]{2,1,0:T(8,128)}, f32[11,192,96]{2,1,0:T(8,128)}, f32[96,768]{1,0:T(8,128)}, f32[96,768]{1,0:T(8,128)}, f32[10,768]{1,0:T(8,128)}...) custom-call(f32[16,768]{1,0:T(8,128)} %get-tuple-element.95.total, f32[8,128]{1,0:T(8,128)} %norm_totals.1.sums, ...), custom_call_target="tpu_custom_call" | custom-call | bytes 7979240 | tf_op jit(solution)/shard_map/lamb_apply/pallas_call | solution.py:495
  397.9 0.0 copy-done.12
  398.0 1.1 copy.40
  (5 shorter events, 0.1 us)
Async XLA Ops:
  369.2 3.6 copy-start
  369.2 3.6 copy-start.1
  369.3 3.5 copy-start.2
  369.3 3.5 copy-start.3
  369.3 3.5 copy-start.4
  369.3 3.5 copy-start.5
  369.3 3.5 copy-start.6
  369.3 3.5 copy-start.7
  369.3 3.5 copy-start.8
  380.8 0.7 copy-start.9
  381.5 0.7 copy-start.10
  382.2 0.5 copy-start.11
  393.0 4.9 %copy-start.12 = (bf16[1024,768]{1,0:T(8,128)(2,1)S(1)}, bf16[1024,768]{1,0:T(8,128)(2,1)}, u32[]{:S(2)}) copy-start(bf16[1024,768]{1,0:T(8,128)(2,1)} %get-tuple-element.150) | copy-start | bytes 4718596

commit v2 on v1

--- a/solution.py
+++ b/solution.py
@@ -677,14 +677,14 @@
 
         lax.fori_loop(0, ROWS // STEP_ROWS, body, 0)
 
-    def take(self, fn):
+    def take(self, fn, first=0, last=ROWS // STEP_ROWS):
         def body(k, carry):
             r = pl.ds(pl.multiple_of(k * STEP_ROWS, STEP_ROWS), STEP_ROWS)
             self.copy(k).wait_recv()
             fn(r, self.sent[r, :].astype(F32) + self.got[r, :].astype(F32))
             return carry
 
-        lax.fori_loop(0, ROWS // STEP_ROWS, body, 0)
+        lax.fori_loop(first, last, body, 0)
 
     def wait_send(self):
         for k in range(ROWS // STEP_ROWS):
@@ -818,7 +818,6 @@
         self.far_out, self.far_in = far_out, far_in
         x, core, z, y = place()
         count = ROWS // 2
-        self.mine = pl.ds(pl.multiple_of(core * count, count), count)
         self.theirs = pl.ds(pl.multiple_of((1 - core) * count, count), count)
         self.sibling, self.across = device(x, 1 - core, z, y), device(1 - x, core, z, y)
 
@@ -829,40 +828,59 @@
         else:
             self.own = copy
 
+    def block(self, j):
+        count = ROWS // 4
+        core = place()[1]
+        return pl.ds(pl.multiple_of(2 * count * core + count * j, count), count), pl.ds(count * j, count)
+
     def cross(self):
         self.other.wait_recv()
-        add_rows(self.far_out, [self.part.at[1, self.mine, :], self.near.at[1]], 64)
-        self.far = self.net.start(self.far_out, self.far_in, self.across)
+        self.far = []
+        for j in range(2):
+            mine, here = self.block(j)
+            add_rows(self.far_out.at[here, :], [self.part.at[1, mine, :], self.near.at[1, here, :]], 64)
+            self.far.append(
+                self.net.start(self.far_out.at[here, :], self.far_in.at[here, :], self.across)
+            )
 
     def end(self):
         self.own.wait_recv()
-        self.far.wait_recv()
-        mine = self.done.at[self.mine, :]
-        add_rows(mine, [self.part.at[0, self.mine, :], self.near.at[0], self.far_in], 64)
-        self.last = self.net.start(mine, mine, self.sibling)
-        self.last.wait_recv()
+        last = []
+        for j in range(2):
+            mine, here = self.block(j)
+            self.far[j].wait_recv()
+            target = self.done.at[mine, :]
+            add_rows(
+                target, [self.part.at[0, mine, :], self.near.at[0, here, :], self.far_in.at[here, :]], 64
+            )
+            last.append(self.net.start(target, target, self.sibling))
+        for copy in last:
+            copy.wait_recv()
 
 
 class Share:
     def __init__(self, net, both, first):
-        self.net, self.both = net, both
+        self.net, self.both, self.far, self.near = net, both, [], []
         x, core, z, y = place()
-        count = ROWS // 2
-        self.mine = pl.ds(pl.multiple_of(first + core * count, TIME), count)
+        count = ROWS // 4
+        self.rows = [
+            pl.ds(pl.multiple_of(first + count * (2 * j + core), TIME), count) for j in range(2)
+        ]
         self.sibling, self.across = device(x, 1 - core, z, y), device(1 - x, core, z, y)
 
-    def begin(self):
-        self.far = self.net.start(
-            self.both.at[0, self.mine, :], self.both.at[1, self.mine, :], self.across
-        )
+    def begin(self, j):
+        r = self.rows[j]
+        self.far.append(self.net.start(self.both.at[0, r, :], self.both.at[1, r, :], self.across))
 
     def pass_on(self):
-        self.far.wait_recv()
-        rows = self.both.at[1, self.mine, :]
-        self.near = self.net.start(rows, rows, self.sibling)
+        for j in range(2):
+            self.far[j].wait_recv()
+            rows = self.both.at[1, self.rows[j], :]
+            self.near.append(self.net.start(rows, rows, self.sibling))
 
     def end(self):
-        self.near.wait_recv()
+        for copy in self.near:
+            copy.wait_recv()
 
 
 def matrix_of(ref, i, first, last):
@@ -887,7 +905,7 @@
     heads = n // HD
     score_scale = HD ** (-0.5)
     net = Sender(send, recv)
-    run = Gather(pieces, held, (2, 4, 0, 0, 0), (3,), net)
+    run = Gather(pieces, held, (2, 3, 0, 0, 0), (3,), net)
     share = Share(net, pad, TIME)
     total_sum = FourSum(net, part, near, far_out, far_in, summed)
     x, core, z, y = place()
@@ -1032,8 +1050,9 @@
         pad[0, moved, :] = (v * jax.nn.sigmoid(v)).astype(LOW)
         return carry
 
-    lax.fori_loop(0, ROWS // STEP_ROWS, act, 0)
-    share.begin()
+    for j in range(2):
+        lax.fori_loop(2 * j, 2 * j + 2, act, 0)
+        share.begin(j)
     run.relay(4)
     local[2].wait()
     run.ready(2)
@@ -1152,7 +1171,7 @@
     ]
     groups = [(2 - (g in (2, 3)), 4, 2, rows, w) for g, w in enumerate(widths)]
     dma = pltpu.SemaphoreType.DMA
-    copies = 3 * 13 + 7 + 4 + 12 + 2 + 4
+    copies = 3 * 13 + 7 + 4 + 12 + 4 + 6
     res = pl.pallas_call(
         forward_body,
         name="forward",
@@ -1427,8 +1446,9 @@
         rows[8:9, :] += gain
         rows[9:10, :] += shift
 
-    sends[0].take(pull_three)
-    share.begin()
+    for j in range(2):
+        sends[0].take(pull_three, 2 * j, 2 * j + 2)
+        share.begin(j)
     tok_load = load(tokens.at[own, :], cot)
     noisy_load = load(noisy_h, resid)
     n2_load = load(n2_h, nrm)
@@ -1547,7 +1567,8 @@
         grad[r, :] = v
         low_grad[r, :] = v.astype(LOW)
 
-    share.far.wait_send()
+    for c in share.far:
+        c.wait_send()
     each_rows(pull_two)
     resid_load = load(resid_h, resid)
     n2_load.wait()
@@ -1679,7 +1700,7 @@
     x_near.wait_recv()
     store_x.wait()
     out_own.wait()
-    wait_sends(net, [sends[0], share.far, *cro.sent])
+    wait_sends(net, [sends[0], *share.far, *cro.sent])
 
 
 def wait_sends(net, done):
@@ -1710,7 +1731,7 @@
     def pieces(width, *counts):
         return [VM((*(k if isinstance(k, tuple) else (k,)), rows, width), LOW) for k in counts]
 
-    copies = 2 + 12 + 2 + 2 + 4 + 5 + 5 + 4 + 4 + parts * 9 + 9
+    copies = 2 + 12 + 4 + 2 + 6 + 5 + 5 + 4 + 4 + parts * 9 + 9
     res = pl.pallas_call(
         backward_body,
         name="backward",

time: 406 us -> 404 us (level)
  no operation moved by 1% of the time
where the time goes in v2:
time: 404 us; the launch traced here: 397 us
  Pallas kernels  387 us (96%)
  other arithmetic  4.97 us (1%)
    pallas_call x1, Pallas kernels, backward_all(): pl.pallas_call(backward_body, name='backward', in_specs=[spec_vm() for _...  193 us
    pallas_call x1, Pallas kernels, forward_all(): pl.pallas_call(forward_body, name='forward', in_specs=[spec_vm() for _ in...  169 us
    pallas_call x1, Pallas kernels, lamb_all(): pl.pallas_call(totals_body, name='norm_totals', in_specs=[spec_vm()], out...  11.7 us

profile of v2, /device:TPU:0, one launch (start us, length us, event | category | flops | bytes accessed | tf_op | source)
XLA Modules:
  0.0 397.2 jit_solution(7184130416818246830)
XLA Ops:
  0.7 0.7 rev.3
  1.4 0.7 fusion.2
  2.2 0.1 multiply_sine_fusion
  2.4 0.7 select_select_fusion
  3.1 169.0 %forward.1 = (bf16[2,4,2,96,768]{4,3,2,1,0:T(8,128)(2,1)}, bf16[2,4,2,96,1536]{4,3,2,1,0:T(8,128)(2,1)}, bf16[1,4,2,96,1920]{4,3,2,1,0:T(8,128)(2,1)}, bf16[1,4,...) custom-call(f32[16,96,192]{2,1,0:T(8,128)} %w_in.3, ...), custom_call_target="tpu_custom_call" | custom-call | tf_op jit(solution)/shard_map/forward/pallas_call | solution.py:1175
  172.1 193.4 %backward.1 = (f32[96,768]{1,0:T(8,128)}, f32[3,96,512]{2,1,0:T(8,128)}, f32[96,1920]{1,0:T(8,128)}, f32[96,1792]{1,0:T(8,128)}, f32[96,768]{1,0:T(8,128)}, /*in...) custom-call(s32[2,512]{1,0:T(2,128)} %segments.3, f32[10,768]{1,0:T(8,128)} %norms.5, ...), custom_call_target="tpu_custom_call" | custom-call | tf_op jit(solution)/shard_map/backward/pallas_call | solution.py:1735
  365.4 0.0 copy-start
  365.5 0.0 copy-start.1
  365.5 0.0 copy-start.2
  365.5 0.0 copy-start.3
  365.5 0.0 copy-start.4
  365.5 0.0 copy-start.5
  365.5 0.0 copy-start.6
  365.5 0.0 copy-start.7
  365.5 0.0 copy-start.8
  365.5 3.5 convert_element_type.19
  369.0 0.0 copy-done
  369.0 0.0 copy-done.1
  369.0 0.0 copy-done.2
  369.0 0.0 copy-done.3
  369.0 0.0 copy-done.4
  369.0 0.0 copy-done.5
  369.0 0.0 copy-done.6
  369.1 0.0 copy-done.7
  369.1 0.0 copy-done.8
  369.1 7.9 %lamb_moments.1 = (f32[16,96,192]{2,1,0:T(8,128)}, f32[11,192,96]{2,1,0:T(8,128)}, f32[96,768]{1,0:T(8,128)}, f32[96,768]{1,0:T(8,128)}, f32[16,96,192]{2,1,0:T(...) custom-call(f32[96,768]{1,0:T(8,128)S(1)} %copy-done.7, ...), custom_call_target="tpu_custom_call" | custom-call | flops 20000000 | bytes 21000000 | tf_op jit(solution)/shard_map/lamb_moments/pallas_call | solution.py:1906
  377.0 0.0 copy-start.9
  377.0 0.7 copy-done.9
  377.7 0.0 copy-start.10
  377.7 0.7 copy-done.10
  378.4 0.0 copy-start.11
  378.4 0.5 copy-done.11
  378.9 11.7 %norm_totals.1.sums = f32[8,128]{1,0:T(8,128)} custom-call(f32[1,128]{1,0:T(1,128)} %copy-done.11), custom_call_target="tpu_custom_call" | custom-call | tf_op jit(solution)/shard_map/norm_totals/pallas_call | solution.py:1921
  390.7 0.0 copy-start.12
  390.7 4.9 %lamb_apply.1 = (f32[16,96,192]{2,1,0:T(8,128)}, f32[11,192,96]{2,1,0:T(8,128)}, f32[96,768]{1,0:T(8,128)}, f32[96,768]{1,0:T(8,128)}, f32[10,768]{1,0:T(8,128)}...) custom-call(f32[16,768]{1,0:T(8,128)} %get-tuple-element.95.total, f32[8,128]{1,0:T(8,128)} %norm_totals.1.sums, ...), custom_call_target="tpu_custom_call" | custom-call | bytes 7979240 | tf_op jit(solution)/shard_map/lamb_apply/pallas_call | solution.py:495
  395.6 0.0 copy-done.12
  395.6 1.1 copy.40
  (5 shorter events, 0.1 us)
Async XLA Ops:
  365.4 3.6 copy-start
  365.5 3.6 copy-start.1
  365.5 3.5 copy-start.2
  365.5 3.5 copy-start.3
  365.5 3.5 copy-start.4
  365.5 3.5 copy-start.5
  365.5 3.5 copy-start.6
  365.5 3.5 copy-start.7
  365.5 3.5 copy-start.8
  377.0 0.7 copy-start.9
  377.7 0.7 copy-start.10
  378.4 0.5 copy-start.11
  390.7 4.9 %copy-start.12 = (bf16[1024,768]{1,0:T(8,128)(2,1)S(1)}, bf16[1024,768]{1,0:T(8,128)(2,1)}, u32[]{:S(2)}) copy-start(bf16[1024,768]{1,0:T(8,128)(2,1)} %get-tuple-element.150) | copy-start | bytes 4718596
